TPU v7x, 32 devices: a whole 2x2x4 slice. The times are simulated.
32 devices in a mesh: dp: 4 (over y, core), shard: 8 (over z, x).
Axes of the slice: x: 2, y: 2, z: 4, core: 2. Of those that a mesh axis runs over, the one named last changes fastest.
Arguments:
- inputs: bfloat16 [2, 32, 512, 768], P(None, ('dp', 'shard')), may hold values from -6 to 6
- doc_ids: int32 [2, 32, 512], P(None, ('dp', 'shard')), may hold values from -1 to 7, as said below
- first_gain: bfloat16 [768], P(('dp', 'shard')), may hold values from 0.5 to 1.5
- first_shift: bfloat16 [768], P(('dp', 'shard')), may hold values from -1.5 to 1.5
- query_weight: bfloat16 [768, 768], P(('dp', 'shard')), may hold values from -0.21875 to 0.21875
- query_bias: bfloat16 [768], P(('dp', 'shard')), may hold values from -1.5 to 1.5
- key_weight: bfloat16 [768, 768], P(('dp', 'shard')), may hold values from -0.21875 to 0.21875
- value_weight: bfloat16 [768, 768], P(('dp', 'shard')), may hold values from -0.21875 to 0.21875
- value_bias: bfloat16 [768], P(('dp', 'shard')), may hold values from -1.5 to 1.5
- second_gain: bfloat16 [768], P(('dp', 'shard')), may hold values from 0.5 to 1.5
- second_shift: bfloat16 [768], P(('dp', 'shard')), may hold values from -1.5 to 1.5
- output_weight: bfloat16 [768, 768], P(('dp', 'shard')), may hold values from -0.21875 to 0.21875
- output_bias: bfloat16 [768], P(('dp', 'shard')), may hold values from -1.5 to 1.5
- third_gain: bfloat16 [768], P(('dp', 'shard')), may hold values from 0.5 to 1.5
- third_shift: bfloat16 [768], P(('dp', 'shard')), may hold values from -1.5 to 1.5
- up_weight: bfloat16 [768, 3072], P(('dp', 'shard')), may hold values from -0.21875 to 0.21875
- up_bias: bfloat16 [3072], P(('dp', 'shard')), may hold values from -1.5 to 1.5
- fourth_gain: bfloat16 [3072], P(('dp', 'shard')), may hold values from 0.5 to 1.5
- fourth_shift: bfloat16 [3072], P(('dp', 'shard')), may hold values from -1.5 to 1.5
- down_weight: bfloat16 [3072, 768], P(('dp', 'shard')), may hold values from -0.109375 to 0.109375
- down_bias: bfloat16 [768], P(('dp', 'shard')), may hold values from -1.5 to 1.5
- cotangent: bfloat16 [2, 32, 512, 768], P(None, ('dp', 'shard')), may hold values from -6 to 6
Outputs:
- layer_out: bfloat16 [2, 32, 512, 768], P(None, ('dp', 'shard'))
- input_grad: bfloat16 [2, 32, 512, 768], P(None, ('dp', 'shard'))
- first_gain_grad: float32 [768], P(('dp', 'shard'))
- first_shift_grad: float32 [768], P(('dp', 'shard'))
- query_weight_grad: float32 [768, 768], P(('dp', 'shard'))
- query_bias_grad: float32 [768], P(('dp', 'shard'))
- key_weight_grad: float32 [768, 768], P(('dp', 'shard'))
- value_weight_grad: float32 [768, 768], P(('dp', 'shard'))
- value_bias_grad: float32 [768], P(('dp', 'shard'))
- second_gain_grad: float32 [768], P(('dp', 'shard'))
- second_shift_grad: float32 [768], P(('dp', 'shard'))
- output_weight_grad: float32 [768, 768], P(('dp', 'shard'))
- output_bias_grad: float32 [768], P(('dp', 'shard'))
- third_gain_grad: float32 [768], P(('dp', 'shard'))
- third_shift_grad: float32 [768], P(('dp', 'shard'))
- up_weight_grad: float32 [768, 3072], P(('dp', 'shard'))
- up_bias_grad: float32 [3072], P(('dp', 'shard'))
- fourth_gain_grad: float32 [3072], P(('dp', 'shard'))
- fourth_shift_grad: float32 [3072], P(('dp', 'shard'))
- down_weight_grad: float32 [3072, 768], P(('dp', 'shard'))
- down_bias_grad: float32 [768], P(('dp', 'shard'))
Inputs may be any that keep to these rules, and one draw needn't show every extreme that they name: `doc_ids`: in each row the ids start at 0 and rise by one from document to document; documents hold 64, 128, 256 or 512 tokens, the last one cut by the row's end; then 1 to 64 padding tokens of id -1 overwrite the row's tail; one row of every draw holds eight documents of 64 tokens, the eighth shortened by its padding.
All inputs are finite; a program needn't handle non-finite values.
Results may differ from a plain program's by a relative error of at most 0.014.
Values may be sent and summed in bfloat16 or wider, within the bound.
A program may use at most 320 MiB of HBM per device.

v0:
```python
import math

import jax
import jax.numpy as jnp
from jax import lax
from jax.sharding import PartitionSpec as P

HD = 64


norm_eps = 1e-05


def layer_norm(values, gain, shift):
    center = values - jnp.mean(values, axis=-1, keepdims=True)
    inverse = lax.rsqrt(jnp.mean(center * center, axis=-1, keepdims=True) + norm_eps)
    normed = center * inverse
    return (normed * gain.astype(jnp.float32) + shift.astype(jnp.float32), normed, inverse)


def norm_back(grad_out, gain, normed, inverse):
    scaled = grad_out * gain.astype(jnp.float32)
    grad_in = inverse * (
        scaled
        - jnp.mean(scaled, axis=-1, keepdims=True)
        - normed * jnp.mean(scaled * normed, axis=-1, keepdims=True)
    )
    return (grad_in, jnp.sum(grad_out * normed, axis=0), jnp.sum(grad_out, axis=0))


def contract_rows(left, right):
    return lax.dot_general(
        left, right, (((0,), (0,)), ((), ())), preferred_element_type=jnp.float32
    )


def times_transpose(left, weight):
    return lax.dot_general(
        left, weight, (((1,), (1,)), ((), ())), preferred_element_type=jnp.float32
    )


def gelu_slope(values):
    cumulative = 0.5 * (1.0 + lax.erf(values * 0.7071067811865476))
    density = jnp.exp(-0.5 * values * values) * 0.3989422804014327
    return cumulative + values * density


def row_mask(ids):
    length = ids.shape[0]
    places = lax.broadcasted_iota(jnp.int32, (length, length), 0)
    others = lax.broadcasted_iota(jnp.int32, (length, length), 1)
    return (ids[:, None] == ids[None, :]) & (ids[None, :] >= 0) | (places == others)


def row_scores(query, keys, ids):
    scale = 1.0 / math.sqrt(query.shape[-1])
    scores = jnp.einsum("qhd,khd->hqk", query, keys, preferred_element_type=jnp.float32) * scale
    return jnp.where(row_mask(ids)[None], scores, -1e30)


def attend_row(group):
    query, keys, values, ids = group
    scores = row_scores(query, keys, ids)
    peak = jnp.max(scores, axis=-1, keepdims=True)
    log_total = peak + jnp.log(jnp.sum(jnp.exp(scores - peak), axis=-1, keepdims=True))
    probs = jnp.exp(scores - log_total).astype(jnp.bfloat16)
    mixed = jnp.einsum("hqk,khd->qhd", probs, values, preferred_element_type=jnp.float32)
    return (mixed, log_total[..., 0])


def attend_back(group):
    query, keys, values, grad_mixed, ids, log_total = group
    scale = 1.0 / math.sqrt(query.shape[-1])
    probs = jnp.exp(row_scores(query, keys, ids) - log_total[..., None])
    grad_values = jnp.einsum(
        "hqk,qhd->khd", probs.astype(jnp.bfloat16), grad_mixed, preferred_element_type=jnp.float32
    )
    grad_probs = jnp.einsum("qhd,khd->hqk", grad_mixed, values, preferred_element_type=jnp.float32)
    grad_scores = probs * (grad_probs - jnp.sum(probs * grad_probs, axis=-1, keepdims=True))
    grad_low = grad_scores.astype(jnp.bfloat16)
    grad_query = (
        jnp.einsum("hqk,khd->qhd", grad_low, keys, preferred_element_type=jnp.float32) * scale
    )
    grad_keys = (
        jnp.einsum("hqk,qhd->khd", grad_low, query, preferred_element_type=jnp.float32) * scale
    )
    return (grad_query, grad_keys, grad_values)


def fetch_mixer(group):
    (
        first_gain,
        first_shift,
        query_weight,
        query_bias,
        key_weight,
        value_weight,
        value_bias,
        second_gain,
        second_shift,
        output_weight,
        output_bias,
    ) = group
    return (
        lax.all_gather(first_gain, ("dp", "shard"), axis=0, tiled=True),
        lax.all_gather(first_shift, ("dp", "shard"), axis=0, tiled=True),
        lax.all_gather(query_weight, ("dp", "shard"), axis=0, tiled=True),
        lax.all_gather(query_bias, ("dp", "shard"), axis=0, tiled=True),
        lax.all_gather(key_weight, ("dp", "shard"), axis=0, tiled=True),
        lax.all_gather(value_weight, ("dp", "shard"), axis=0, tiled=True),
        lax.all_gather(value_bias, ("dp", "shard"), axis=0, tiled=True),
        lax.all_gather(second_gain, ("dp", "shard"), axis=0, tiled=True),
        lax.all_gather(second_shift, ("dp", "shard"), axis=0, tiled=True),
        lax.all_gather(output_weight, ("dp", "shard"), axis=0, tiled=True),
        lax.all_gather(output_bias, ("dp", "shard"), axis=0, tiled=True),
    )


def fetch_feed(group):
    (
        third_gain,
        third_shift,
        up_weight,
        up_bias,
        fourth_gain,
        fourth_shift,
        down_weight,
        down_bias,
    ) = group
    return (
        lax.all_gather(third_gain, ("dp", "shard"), axis=0, tiled=True),
        lax.all_gather(third_shift, ("dp", "shard"), axis=0, tiled=True),
        lax.all_gather(up_weight, ("dp", "shard"), axis=0, tiled=True),
        lax.all_gather(up_bias, ("dp", "shard"), axis=0, tiled=True),
        lax.all_gather(fourth_gain, ("dp", "shard"), axis=0, tiled=True),
        lax.all_gather(fourth_shift, ("dp", "shard"), axis=0, tiled=True),
        lax.all_gather(down_weight, ("dp", "shard"), axis=0, tiled=True),
        lax.all_gather(down_bias, ("dp", "shard"), axis=0, tiled=True),
    )


def forward_pass(tokens, ids, mixer_full, feed_full):
    (
        first_gain,
        first_shift,
        query_weight,
        query_bias,
        key_weight,
        value_weight,
        value_bias,
        second_gain,
        second_shift,
        output_weight,
        output_bias,
    ) = mixer_full
    (
        third_gain,
        third_shift,
        up_weight,
        up_bias,
        fourth_gain,
        fourth_shift,
        down_weight,
        down_bias,
    ) = feed_full
    rows, length, width = tokens.shape
    flat = tokens.reshape(rows * length, width).astype(jnp.float32)
    normed_in, first_normed, first_inverse = layer_norm(flat, first_gain, first_shift)
    mixer_in = normed_in.astype(jnp.bfloat16)
    query = (
        jnp.dot(mixer_in, query_weight, preferred_element_type=jnp.float32)
        + query_bias.astype(jnp.float32)
    ).astype(jnp.bfloat16)
    keys = jnp.dot(mixer_in, key_weight, preferred_element_type=jnp.float32).astype(jnp.bfloat16)
    values = (
        jnp.dot(mixer_in, value_weight, preferred_element_type=jnp.float32)
        + value_bias.astype(jnp.float32)
    ).astype(jnp.bfloat16)
    shape_heads = (rows, length, width // HD, HD)
    mixed, log_total = lax.map(
        attend_row,
        (query.reshape(shape_heads), keys.reshape(shape_heads), values.reshape(shape_heads), ids),
    )
    mixed = mixed.reshape(rows * length, width)
    normed_mid, second_normed, second_inverse = layer_norm(mixed, second_gain, second_shift)
    branch_in = normed_mid.astype(jnp.bfloat16)
    residual = (
        flat
        + jnp.dot(branch_in, output_weight, preferred_element_type=jnp.float32)
        + output_bias.astype(jnp.float32)
    )
    normed_feed, third_normed, third_inverse = layer_norm(residual, third_gain, third_shift)
    feed_in = normed_feed.astype(jnp.bfloat16)
    upper = jnp.dot(feed_in, up_weight, preferred_element_type=jnp.float32) + up_bias.astype(
        jnp.float32
    )
    normed_act, fourth_normed, fourth_inverse = layer_norm(
        jax.nn.gelu(upper, approximate=False), fourth_gain, fourth_shift
    )
    down_in = normed_act.astype(jnp.bfloat16)
    result = (
        residual
        + jnp.dot(down_in, down_weight, preferred_element_type=jnp.float32)
        + down_bias.astype(jnp.float32)
    )
    kept = (
        mixer_in,
        query,
        keys,
        values,
        log_total,
        first_normed,
        first_inverse,
        second_normed,
        second_inverse,
        branch_in,
        third_normed,
        third_inverse,
        feed_in,
        upper,
        fourth_normed,
        fourth_inverse,
        down_in,
    )
    return (result.astype(jnp.bfloat16).reshape(tokens.shape), kept)


def backward_pass(grad_out, ids, kept, mixer_full, feed_full):
    (
        first_gain,
        first_shift,
        query_weight,
        query_bias,
        key_weight,
        value_weight,
        value_bias,
        second_gain,
        second_shift,
        output_weight,
        output_bias,
    ) = mixer_full
    (
        third_gain,
        third_shift,
        up_weight,
        up_bias,
        fourth_gain,
        fourth_shift,
        down_weight,
        down_bias,
    ) = feed_full
    (
        mixer_in,
        query,
        keys,
        values,
        log_total,
        first_normed,
        first_inverse,
        second_normed,
        second_inverse,
        branch_in,
        third_normed,
        third_inverse,
        feed_in,
        upper,
        fourth_normed,
        fourth_inverse,
        down_in,
    ) = kept
    rows, length, width = grad_out.shape
    grad_top = grad_out.reshape(rows * length, width).astype(jnp.float32)
    grad_down = grad_top.astype(jnp.bfloat16)
    down_weight_grad = contract_rows(down_in, grad_down)
    down_bias_grad = jnp.sum(grad_down.astype(jnp.float32), axis=0)
    grad_act, fourth_gain_grad, fourth_shift_grad = norm_back(
        times_transpose(grad_down, down_weight), fourth_gain, fourth_normed, fourth_inverse
    )
    grad_upper = (grad_act * gelu_slope(upper)).astype(jnp.bfloat16)
    up_weight_grad = contract_rows(feed_in, grad_upper)
    up_bias_grad = jnp.sum(grad_upper.astype(jnp.float32), axis=0)
    grad_feed, third_gain_grad, third_shift_grad = norm_back(
        times_transpose(grad_upper, up_weight), third_gain, third_normed, third_inverse
    )
    grad_residual = grad_top + grad_feed
    grad_branch = grad_residual.astype(jnp.bfloat16)
    output_weight_grad = contract_rows(branch_in, grad_branch)
    output_bias_grad = jnp.sum(grad_branch.astype(jnp.float32), axis=0)
    grad_mixed, second_gain_grad, second_shift_grad = norm_back(
        times_transpose(grad_branch, output_weight), second_gain, second_normed, second_inverse
    )
    shape_heads = (rows, length, width // HD, HD)
    grad_query, grad_keys, grad_values = lax.map(
        attend_back,
        (
            query.reshape(shape_heads),
            keys.reshape(shape_heads),
            values.reshape(shape_heads),
            grad_mixed.astype(jnp.bfloat16).reshape(shape_heads),
            ids,
            log_total,
        ),
    )
    grad_query = grad_query.reshape(rows * length, width).astype(jnp.bfloat16)
    grad_keys = grad_keys.reshape(rows * length, width).astype(jnp.bfloat16)
    grad_values = grad_values.reshape(rows * length, width).astype(jnp.bfloat16)
    query_weight_grad = contract_rows(mixer_in, grad_query)
    query_bias_grad = jnp.sum(grad_query.astype(jnp.float32), axis=0)
    key_weight_grad = contract_rows(mixer_in, grad_keys)
    value_weight_grad = contract_rows(mixer_in, grad_values)
    value_bias_grad = jnp.sum(grad_values.astype(jnp.float32), axis=0)
    grad_normed = (
        times_transpose(grad_query, query_weight)
        + times_transpose(grad_keys, key_weight)
        + times_transpose(grad_values, value_weight)
    )
    grad_first, first_gain_grad, first_shift_grad = norm_back(
        grad_normed, first_gain, first_normed, first_inverse
    )
    grad_input = (grad_residual + grad_first).astype(jnp.bfloat16).reshape(grad_out.shape)
    mixer_grads = (
        first_gain_grad,
        first_shift_grad,
        query_weight_grad,
        query_bias_grad,
        key_weight_grad,
        value_weight_grad,
        value_bias_grad,
        second_gain_grad,
        second_shift_grad,
        output_weight_grad,
        output_bias_grad,
    )
    feed_grads = (
        third_gain_grad,
        third_shift_grad,
        up_weight_grad,
        up_bias_grad,
        fourth_gain_grad,
        fourth_shift_grad,
        down_weight_grad,
        down_bias_grad,
    )
    return (grad_input, mixer_grads, feed_grads)


def on_device(
    inputs,
    doc_ids,
    first_gain,
    first_shift,
    query_weight,
    query_bias,
    key_weight,
    value_weight,
    value_bias,
    second_gain,
    second_shift,
    output_weight,
    output_bias,
    third_gain,
    third_shift,
    up_weight,
    up_bias,
    fourth_gain,
    fourth_shift,
    down_weight,
    down_bias,
    cotangent,
):
    mixer_own = (
        first_gain,
        first_shift,
        query_weight,
        query_bias,
        key_weight,
        value_weight,
        value_bias,
        second_gain,
        second_shift,
        output_weight,
        output_bias,
    )
    feed_own = (
        third_gain,
        third_shift,
        up_weight,
        up_bias,
        fourth_gain,
        fourth_shift,
        down_weight,
        down_bias,
    )
    devices_all = lax.axis_size("dp") * lax.axis_size("shard")
    mixer_sums = tuple(
        (
            jnp.zeros((piece.shape[0] * devices_all,) + piece.shape[1:], jnp.float32)
            for piece in mixer_own
        )
    )
    feed_sums = tuple(
        (
            jnp.zeros((piece.shape[0] * devices_all,) + piece.shape[1:], jnp.float32)
            for piece in feed_own
        )
    )
    results = []
    input_grads = []
    for batch_index in range(inputs.shape[0]):
        tokens = inputs[batch_index]
        fresh_mixer, fresh_feed, tokens = lax.optimization_barrier((mixer_own, feed_own, tokens))
        mixer_full = fetch_mixer(fresh_mixer)
        feed_full = fetch_feed(fresh_feed)
        result, kept = forward_pass(tokens, doc_ids[batch_index], mixer_full, feed_full)
        fresh_mixer, fresh_feed, kept = lax.optimization_barrier((mixer_own, feed_own, kept))
        mixer_full = fetch_mixer(fresh_mixer)
        feed_full = fetch_feed(fresh_feed)
        grad_input, mixer_grads, feed_grads = backward_pass(
            cotangent[batch_index], doc_ids[batch_index], kept, mixer_full, feed_full
        )
        mixer_sums = jax.tree.map(jnp.add, mixer_sums, mixer_grads)
        feed_sums = jax.tree.map(jnp.add, feed_sums, feed_grads)
        results.append(result)
        input_grads.append(grad_input)
    (
        sum_one,
        sum_two,
        sum_three,
        sum_four,
        sum_five,
        sum_six,
        sum_seven,
        sum_eight,
        sum_nine,
        sum_ten,
        sum_eleven,
    ) = mixer_sums
    mixer_owned = (
        lax.psum_scatter(sum_one, ("dp", "shard"), scatter_dimension=0, tiled=True),
        lax.psum_scatter(sum_two, ("dp", "shard"), scatter_dimension=0, tiled=True),
        lax.psum_scatter(sum_three, ("dp", "shard"), scatter_dimension=0, tiled=True),
        lax.psum_scatter(sum_four, ("dp", "shard"), scatter_dimension=0, tiled=True),
        lax.psum_scatter(sum_five, ("dp", "shard"), scatter_dimension=0, tiled=True),
        lax.psum_scatter(sum_six, ("dp", "shard"), scatter_dimension=0, tiled=True),
        lax.psum_scatter(sum_seven, ("dp", "shard"), scatter_dimension=0, tiled=True),
        lax.psum_scatter(sum_eight, ("dp", "shard"), scatter_dimension=0, tiled=True),
        lax.psum_scatter(sum_nine, ("dp", "shard"), scatter_dimension=0, tiled=True),
        lax.psum_scatter(sum_ten, ("dp", "shard"), scatter_dimension=0, tiled=True),
        lax.psum_scatter(sum_eleven, ("dp", "shard"), scatter_dimension=0, tiled=True),
    )
    feed_one, feed_two, feed_three, feed_four, feed_five, feed_six, feed_seven, feed_eight = (
        feed_sums
    )
    feed_owned = (
        lax.psum_scatter(feed_one, ("dp", "shard"), scatter_dimension=0, tiled=True),
        lax.psum_scatter(feed_two, ("dp", "shard"), scatter_dimension=0, tiled=True),
        lax.psum_scatter(feed_three, ("dp", "shard"), scatter_dimension=0, tiled=True),
        lax.psum_scatter(feed_four, ("dp", "shard"), scatter_dimension=0, tiled=True),
        lax.psum_scatter(feed_five, ("dp", "shard"), scatter_dimension=0, tiled=True),
        lax.psum_scatter(feed_six, ("dp", "shard"), scatter_dimension=0, tiled=True),
        lax.psum_scatter(feed_seven, ("dp", "shard"), scatter_dimension=0, tiled=True),
        lax.psum_scatter(feed_eight, ("dp", "shard"), scatter_dimension=0, tiled=True),
    )
    return (jnp.stack(results), jnp.stack(input_grads)) + tuple(mixer_owned) + tuple(feed_owned)


def solution(mesh):
    placed = (
        P(None, ("dp", "shard"), None, None),
        P(None, ("dp", "shard"), None),
        P(("dp", "shard")),
        P(("dp", "shard")),
        P(("dp", "shard"), None),
        P(("dp", "shard")),
        P(("dp", "shard"), None),
        P(("dp", "shard"), None),
        P(("dp", "shard")),
        P(("dp", "shard")),
        P(("dp", "shard")),
        P(("dp", "shard"), None),
        P(("dp", "shard")),
        P(("dp", "shard")),
        P(("dp", "shard")),
        P(("dp", "shard"), None),
        P(("dp", "shard")),
        P(("dp", "shard")),
        P(("dp", "shard")),
        P(("dp", "shard"), None),
        P(("dp", "shard")),
        P(None, ("dp", "shard"), None, None),
    )
    return jax.shard_map(
        on_device,
        mesh=mesh,
        in_specs=placed,
        out_specs=(
            P(None, ("dp", "shard"), None, None),
            P(None, ("dp", "shard"), None, None),
            P(("dp", "shard")),
            P(("dp", "shard")),
            P(("dp", "shard"), None),
            P(("dp", "shard")),
            P(("dp", "shard"), None),
            P(("dp", "shard"), None),
            P(("dp", "shard")),
            P(("dp", "shard")),
            P(("dp", "shard")),
            P(("dp", "shard"), None),
            P(("dp", "shard")),
            P(("dp", "shard")),
            P(("dp", "shard")),
            P(("dp", "shard"), None),
            P(("dp", "shard")),
            P(("dp", "shard")),
            P(("dp", "shard")),
            P(("dp", "shard"), None),
            P(("dp", "shard")),
        ),
        check_vma=False,
    )
```

profile of v0, /device:TPU:0, one launch (start us, length us, event | category | flops | bytes accessed | tf_op | source)
XLA Modules:
  0.0 2293.9 jit_solution(17325067203287584826)
XLA Ops:
  35.0 44.5 %all-reduce.49 = (bf16[768]{0:T(1024)(128)(2,1)S(1)}, bf16[768]{0:T(1024)(128)(2,1)S(1)}, bf16[768]{0:T(1024)(128)(2,1)S(1)}, bf16[768]{0:T(1024)(128)(2,1)S(1)}...) all-reduce(bf16[768]{0:T(1024)(128)(2,1)S(1)} %dynamic-update-slice, ...), channel_id=1, replica_groups=mesh['dp'=4,'shard'=8] {'dp','shard'}, use_global_device_ids=true, to_apply=%add.14 | all-reduce | flops 32256 | bytes 129024
  85.5 38.4 %all-gather.39.cloned.1.call-done = bf16[768,768]{1,0:T(8,128)(2,1)} async-done(((bf16[24,768]{1,0:T(8,128)(2,1)}), bf16[768,768]{1,0:T(8,128)(2,1)}) %all-gather.39.cloned.1.call-update) | async-done | bytes 1179664 | tf_op jit(solution)/shard_map/all_gather | solution.py:108
  128.3 51.7 %all-gather.41.cloned.1.call-done = bf16[768,768]{1,0:T(8,128)(2,1)} async-done(((bf16[24,768]{1,0:T(8,128)(2,1)}), bf16[768,768]{1,0:T(8,128)(2,1)}) %all-gather.41.cloned.1.call-update) | async-done | bytes 1179664 | tf_op jit(solution)/shard_map/all_gather | solution.py:110
  240.8 60.4 %all-gather.45.cloned.1.call-done = bf16[768,3072]{1,0:T(8,128)(2,1)} async-done(((bf16[24,3072]{1,0:T(8,128)(2,1)}), bf16[768,3072]{1,0:T(8,128)(2,1)}) %all-gather.45.cloned.1.call-update) | async-done | bytes 4718608 | tf_op jit(solution)/shard_map/all_gather | solution.py:134
  358.9 53.6 %all-gather.29.cloned.1.call-done = bf16[768,768]{1,0:T(8,128)(2,1)} async-done(((bf16[24,768]{1,0:T(8,128)(2,1)}), bf16[768,768]{1,0:T(8,128)(2,1)}) %all-gather.29.cloned.1.call-update) | async-done | bytes 1179664 | tf_op jit(solution)/shard_map/all_gather | solution.py:110
  416.9 51.6 %all-gather.25.cloned.1.call-done = bf16[768,768]{1,0:T(8,128)(2,1)} async-done(((bf16[24,768]{1,0:T(8,128)(2,1)}), bf16[768,768]{1,0:T(8,128)(2,1)}) %all-gather.25.cloned.1.call-update) | async-done | bytes 1179664 | tf_op jit(solution)/shard_map/all_gather | solution.py:111
  529.3 60.6 %all-gather.33.cloned.1.call-done = bf16[768,3072]{1,0:T(8,128)(2,1)} async-done(((bf16[24,3072]{1,0:T(8,128)(2,1)}), bf16[768,3072]{1,0:T(8,128)(2,1)}) %all-gather.33.cloned.1.call-update) | async-done | bytes 4718608 | tf_op jit(solution)/shard_map/all_gather | solution.py:134
  623.9 40.1 %all-reduce.48 = (bf16[768]{0:T(1024)(128)(2,1)}, bf16[768]{0:T(1024)(128)(2,1)}, bf16[3072]{0:T(1024)(128)(2,1)S(1)}, bf16[768]{0:T(1024)(128)(2,1)S(1)}, bf16[...) all-reduce(bf16[768]{0:T(1024)(128)(2,1)S(1)} %dynamic-update-slice, ...), channel_id=1, replica_groups=mesh['dp'=4,'shard'=8] {'dp','shard'}, use_global_device_ids=true, to_apply=%add.25 | all-reduce | flops 12288 | bytes 49152
  727.4 57.5 %all-gather.49.cloned.1.call-done = bf16[3072,768]{1,0:T(8,128)(2,1)} async-done(((bf16[96,768]{1,0:T(8,128)(2,1)}), bf16[3072,768]{1,0:T(8,128)(2,1)}) %all-gather.49.cloned.1.call-update) | async-done | bytes 4718608 | tf_op jit(solution)/shard_map/all_gather | solution.py:138
  802.8 46.9 %all-gather.51.cloned.1.call-done = bf16[768,3072]{1,0:T(8,128)(2,1)} async-done(((bf16[24,3072]{1,0:T(8,128)(2,1)}), bf16[768,3072]{1,0:T(8,128)(2,1)}) %all-gather.51.cloned.1.call-update) | async-done | bytes 4718608 | tf_op jit(solution)/shard_map/all_gather | solution.py:134
  858.0 47.1 %all-gather.65.cloned.1.call-done = bf16[768,768]{1,0:T(8,128)(2,1)} async-done(((bf16[24,768]{1,0:T(8,128)(2,1)}), bf16[768,768]{1,0:T(8,128)(2,1)}) %all-gather.65.cloned.1.call-update) | async-done | bytes 1179664 | tf_op jit(solution)/shard_map/all_gather | solution.py:115
  1033.6 39.0 %all-gather.69.cloned.1.call-done = bf16[768,768]{1,0:T(8,128)(2,1)} async-done(((bf16[24,768]{1,0:T(8,128)(2,1)}), bf16[768,768]{1,0:T(8,128)(2,1)}) %all-gather.69.cloned.1.call-update) | async-done | bytes 1179664 | tf_op jit(solution)/shard_map/all_gather | solution.py:110
  1076.1 52.5 %all-gather.55.cloned.1.call-done = bf16[768,768]{1,0:T(8,128)(2,1)} async-done(((bf16[24,768]{1,0:T(8,128)(2,1)}), bf16[768,768]{1,0:T(8,128)(2,1)}) %all-gather.55.cloned.1.call-update) | async-done | bytes 1179664 | tf_op jit(solution)/shard_map/all_gather | solution.py:108
  1138.0 46.4 %all-gather.57.cloned.1.call-done = bf16[768,768]{1,0:T(8,128)(2,1)} async-done(((bf16[24,768]{1,0:T(8,128)(2,1)}), bf16[768,768]{1,0:T(8,128)(2,1)}) %all-gather.57.cloned.1.call-update) | async-done | bytes 1179664 | tf_op jit(solution)/shard_map/all_gather | solution.py:110
  1188.0 52.5 %all-gather.71.cloned.1.call-done = bf16[768,768]{1,0:T(8,128)(2,1)} async-done(((bf16[24,768]{1,0:T(8,128)(2,1)}), bf16[768,768]{1,0:T(8,128)(2,1)}) %all-gather.71.cloned.1.call-update) | async-done | bytes 1179664 | tf_op jit(solution)/shard_map/all_gather | solution.py:111
  1245.8 50.7 %all-gather.59.cloned.1.call-done = bf16[768,768]{1,0:T(8,128)(2,1)} async-done(((bf16[24,768]{1,0:T(8,128)(2,1)}), bf16[768,768]{1,0:T(8,128)(2,1)}) %all-gather.59.cloned.1.call-update) | async-done | bytes 1179664 | tf_op jit(solution)/shard_map/all_gather | solution.py:111
  1369.2 57.6 %all-gather.35.cloned.1.call-done = bf16[3072,768]{1,0:T(8,128)(2,1)} async-done(((bf16[96,768]{1,0:T(8,128)(2,1)}), bf16[3072,768]{1,0:T(8,128)(2,1)}) %all-gather.35.cloned.1.call-update) | async-done | bytes 4718608 | tf_op jit(solution)/shard_map/all_gather | solution.py:138
  1437.4 142.3 %all-reduce.52.cloned.1.call-done = (f32[768]{0:T(1024)}, f32[768]{0:T(1024)}, f32[768]{0:T(1024)}, f32[768]{0:T(1024)}, f32[768]{0:T(1024)}, /*index=5*/f32[768...) async-done(((f32[768]{0:T(1024)}, f32[768]{0:T(1024)}, f32[768]{0:T(1024)}, ...) | async-done | bytes 67600
  1596.1 94.2 %reduce-scatter.7.cloned.1.call-done = f32[24,768]{1,0:T(8,128)} async-done(((f32[768,768]{1,0:T(8,128)}), f32[24,768]{1,0:T(8,128)}) %reduce-scatter.7.cloned.1.call-update) | async-done | bytes 73744 | tf_op jit(solution)/shard_map/reduce_scatter | solution.py:442
  1690.3 104.4 %reduce-scatter.9.cloned.1.call-done = f32[24,768]{1,0:T(8,128)} async-done(((f32[768,768]{1,0:T(8,128)}), f32[24,768]{1,0:T(8,128)}) %reduce-scatter.9.cloned.1.call-update) | async-done | bytes 73744 | tf_op jit(solution)/shard_map/reduce_scatter | solution.py:444
  1794.7 104.5 %reduce-scatter.11.cloned.1.call-done = f32[24,768]{1,0:T(8,128)} async-done(((f32[768,768]{1,0:T(8,128)}), f32[24,768]{1,0:T(8,128)}) %reduce-scatter.11.cloned.1.call-update) | async-done | bytes 73744 | tf_op jit(solution)/shard_map/reduce_scatter | solution.py:445
  1899.2 104.5 %reduce-scatter.13.cloned.1.call-done = f32[24,768]{1,0:T(8,128)} async-done(((f32[768,768]{1,0:T(8,128)}), f32[24,768]{1,0:T(8,128)}) %reduce-scatter.13.cloned.1.call-update) | async-done | bytes 73744 | tf_op jit(solution)/shard_map/reduce_scatter | solution.py:449
  2003.7 141.5 %reduce-scatter.17.cloned.1.call-done = f32[96,768]{1,0:T(8,128)} async-done(((f32[3072,768]{1,0:T(8,128)}), f32[96,768]{1,0:T(8,128)}) %reduce-scatter.17.cloned.1.call-update) | async-done | bytes 294928 | tf_op jit(solution)/shard_map/reduce_scatter | solution.py:462
  2145.2 141.7 %reduce-scatter.15.cloned.1.call-done = f32[24,3072]{1,0:T(8,128)} async-done(((f32[768,3072]{1,0:T(8,128)}), f32[24,3072]{1,0:T(8,128)}) %reduce-scatter.15.cloned.1.call-update) | async-done | bytes 294928 | tf_op jit(solution)/shard_map/reduce_scatter | solution.py:458
  (524 shorter events, 593.5 us)
Async XLA Ops:
  11.4 345.1 %all-gather.27.cloned.1.call-start = ((), (), s32[]{:S(2)}) async-start(), calls=%async_computation.7 | async-start | bytes 1216512 | tf_op jit(solution)/shard_map/all_gather | solution.py:108
  12.0 400.5 %all-gather.29.cloned.1.call-start = ((), (), s32[]{:S(2)}) async-start(), calls=%async_computation.8 | async-start | bytes 1216512 | tf_op jit(solution)/shard_map/all_gather | solution.py:110
  12.7 455.8 %all-gather.25.cloned.1.call-start = ((), (), s32[]{:S(2)}) async-start(), calls=%async_computation.6 | async-start | bytes 1216512 | tf_op jit(solution)/shard_map/all_gather | solution.py:111
  13.5 511.1 %all-gather.31.cloned.1.call-start = ((), (), s32[]{:S(2)}) async-start(), calls=%async_computation.9 | async-start | bytes 1216512 | tf_op jit(solution)/shard_map/all_gather | solution.py:115
  14.2 575.7 %all-gather.33.cloned.1.call-start = ((), (), s32[]{:S(2)}) async-start(), calls=%async_computation.10 | async-start | bytes 4866048 | tf_op jit(solution)/shard_map/all_gather | solution.py:134
  14.8 669.5 %all-gather.61.cloned.1.call-start = ((), (), s32[]{:S(2)}) async-start(), calls=%async_computation.24 | async-start | bytes 4866048 | tf_op jit(solution)/shard_map/all_gather | solution.py:138
  326.0 394.0 %all-gather.63.cloned.1.call-start = ((), (), s32[]{:S(2)}) async-start(), calls=%async_computation.25 | async-start | bytes 4866048 | tf_op jit(solution)/shard_map/all_gather | solution.py:134
  479.5 305.5 %all-gather.49.cloned.1.call-start = ((), (), s32[]{:S(2)}) async-start(), calls=%async_computation.18 | async-start | bytes 4866048 | tf_op jit(solution)/shard_map/all_gather | solution.py:138
  615.7 345.2 %all-gather.53.cloned.1.call-start = ((), (), s32[]{:S(2)}) async-start(), calls=%async_computation.20 | async-start | bytes 1216512 | tf_op jit(solution)/shard_map/all_gather | solution.py:115
  616.3 407.9 %all-gather.67.cloned.1.call-start = ((), (), s32[]{:S(2)}) async-start(), calls=%async_computation.27 | async-start | bytes 1216512 | tf_op jit(solution)/shard_map/all_gather | solution.py:108
  616.9 455.7 %all-gather.69.cloned.1.call-start = ((), (), s32[]{:S(2)}) async-start(), calls=%async_computation.28 | async-start | bytes 1216512 | tf_op jit(solution)/shard_map/all_gather | solution.py:110
  617.5 511.1 %all-gather.55.cloned.1.call-start = ((), (), s32[]{:S(2)}) async-start(), calls=%async_computation.21 | async-start | bytes 1216512 | tf_op jit(solution)/shard_map/all_gather | solution.py:108
  618.2 566.2 %all-gather.57.cloned.1.call-start = ((), (), s32[]{:S(2)}) async-start(), calls=%async_computation.22 | async-start | bytes 1216512 | tf_op jit(solution)/shard_map/all_gather | solution.py:110
  618.8 621.7 %all-gather.71.cloned.1.call-start = ((), (), s32[]{:S(2)}) async-start(), calls=%async_computation.29 | async-start | bytes 1216512 | tf_op jit(solution)/shard_map/all_gather | solution.py:111
  619.6 676.9 %all-gather.59.cloned.1.call-start = ((), (), s32[]{:S(2)}) async-start(), calls=%async_computation.23 | async-start | bytes 1216512 | tf_op jit(solution)/shard_map/all_gather | solution.py:111
  620.3 741.6 %all-gather.47.cloned.1.call-start = ((), (), s32[]{:S(2)}) async-start(), calls=%async_computation.17 | async-start | bytes 4866048 | tf_op jit(solution)/shard_map/all_gather | solution.py:138
  621.0 805.7 %all-gather.35.cloned.1.call-start = ((), (), s32[]{:S(2)}) async-start(), calls=%async_computation.11 | async-start | bytes 4866048 | tf_op jit(solution)/shard_map/all_gather | solution.py:138
  621.6 958.1 %all-reduce.52.cloned.1.call-start = ((), (), s32[]{:S(2)}) async-start(), calls=%async_computation.36 | async-start | bytes 155648
  1312.0 378.3 %reduce-scatter.7.cloned.1.call-start = ((), (), s32[]{:S(2)}) async-start(), calls=%async_computation.30 | async-start | bytes 2433024 | tf_op jit(solution)/shard_map/reduce_scatter | solution.py:442
  1316.5 478.2 %reduce-scatter.9.cloned.1.call-start = ((), (), s32[]{:S(2)}) async-start(), calls=%async_computation.31 | async-start | bytes 2433024 | tf_op jit(solution)/shard_map/reduce_scatter | solution.py:444
  1322.3 576.8 %reduce-scatter.11.cloned.1.call-start = ((), (), s32[]{:S(2)}) async-start(), calls=%async_computation.32 | async-start | bytes 2433024 | tf_op jit(solution)/shard_map/reduce_scatter | solution.py:445
  1328.5 675.2 %reduce-scatter.13.cloned.1.call-start = ((), (), s32[]{:S(2)}) async-start(), calls=%async_computation.33 | async-start | bytes 2433024 | tf_op jit(solution)/shard_map/reduce_scatter | solution.py:449
  1332.8 812.4 %reduce-scatter.17.cloned.1.call-start = ((), (), s32[]{:S(2)}) async-start(), calls=%async_computation.35 | async-start | bytes 9732096 | tf_op jit(solution)/shard_map/reduce_scatter | solution.py:462
  1343.3 943.6 %reduce-scatter.15.cloned.1.call-start = ((), (), s32[]{:S(2)}) async-start(), calls=%async_computation.34 | async-start | bytes 9732096 | tf_op jit(solution)/shard_map/reduce_scatter | solution.py:458
  (99 other events, 3809.6 us)
Sparse Core Ops, SparseCore 0:
  11.0 56.8 all-gather.36
  70.9 53.0 all-gather.38
  127.0 52.9 all-gather.40
  182.8 52.9 all-gather.42
  238.7 62.5 all-gather.44
  359.5 52.9 all-gather.28
  527.4 62.5 all-gather.32
  592.9 62.3 all-gather.60
  658.1 61.8 all-gather.62
  723.0 61.9 all-gather.48
  787.8 61.9 all-gather.50
  907.9 52.9 all-gather.52
  963.7 52.9 all-gather.66
  1019.6 52.9 all-gather.68
  1131.5 52.9 all-gather.56
  1299.5 62.4 all-gather.46
  1364.8 61.9 all-gather.34
  1433.2 146.4 all-reduce.51
  1587.6 102.6 reduce-scatter.6
  1696.0 98.6 reduce-scatter.8
  1800.6 98.5 reduce-scatter.10
  1905.1 98.5 reduce-scatter.12
  2010.0 135.1 reduce-scatter.16
  2151.7 135.1 reduce-scatter.14
  (7 shorter events, 369.3 us)
where the time goes:
time: 2300 us; the launch traced here: 2290 us
  waiting for transfers between devices  1750 us (76%)
  matrix products  270 us (12%)
  other arithmetic  89.3 us (4%)
  blocking collectives  84.6 us (4%)
  local copies, waits for them, and re-layouts  78.1 us (3%)
    all_gather x4, waiting for transfers between devices, fetch_mixer(): lax.all_gather(key_weight, ('dp', 'shard'), axis=0, tiled=True)  191 us
    all_gather x4, waiting for transfers between devices, fetch_feed(): lax.all_gather(up_weight, ('dp', 'shard'), axis=0, tiled=True)  185 us
    all_gather x4, waiting for transfers between devices, fetch_mixer(): lax.all_gather(value_weight, ('dp', 'shard'), axis=0, tiled=True)  155 us
    unnamed x32, waiting for transfers between devices  154 us
    reduce_scatter x1, waiting for transfers between devices, on_device(): lax.psum_scatter(feed_three, ('dp', 'shard'), scatter_dimension=0, tiled=...  142 us
    reduce_scatter x1, waiting for transfers between devices, on_device(): lax.psum_scatter(feed_seven, ('dp', 'shard'), scatter_dimension=0, tiled=...  142 us
    all_gather x4, waiting for transfers between devices, fetch_mixer(): lax.all_gather(output_weight, ('dp', 'shard'), axis=0, tiled=True)  138 us
    all_gather x4, waiting for transfers between devices, fetch_feed(): lax.all_gather(down_weight, ('dp', 'shard'), axis=0, tiled=True)  123 us
  transfers between devices with their start and end apart: 31, of which 28 were waited for; matrix products, arithmetic and copies ran while one was open for 18% of the time, Pallas kernels for 0%

commit v1 on v0

v1 whole, which is shorter than its diff:
```python
import functools

import jax
import jax.numpy as jnp
from jax import lax
from jax.experimental import pallas as pl
from jax.experimental.pallas import tpu as pltpu
from jax.sharding import PartitionSpec as P


MESH = pl.DeviceIdType.MESH
AXES = ("dp", "shard")


class Grid:
    def __init__(self, dp, shard):
        self.ny = dp // 2
        self.nx = self.ny
        self.nz = shard // self.nx

    def here(self):
        dp, shard = lax.axis_index("dp"), lax.axis_index("shard")
        return dp // 2, dp % 2, shard // self.nx, shard % self.nx

    def device(self, y, c, z, x):
        return (y * 2 + c, z * self.nx + x)

    def blocks(self):
        return (self.ny, 2, self.nz, self.nx)


def others(size, mine):
    return [lax.rem(mine + k, size) for k in range(1, size)]


def greet(grid, y, c, z, x):
    barrier = pltpu.get_barrier_semaphore()
    peers = (
        [(y, c, p, x) for p in others(grid.nz, z)]
        + [(y, c, z, p) for p in others(grid.nx, x)]
        + [(p, c, z, x) for p in others(grid.ny, y)]
        + [(y, 1 - c, z, x)]
    )
    for peer in peers:
        pl.semaphore_signal(barrier, inc=1, device_id=grid.device(*peer), device_id_type=MESH)
    pl.semaphore_wait(barrier, len(peers))


class Gather:
    def __init__(self, grid, place, source, target, colour, send, recv, local):
        self.g, self.place = grid, place
        self.source, self.target, self.colour = source, target, colour
        self.send, self.recv, self.local = send, recv, local

    def plan(self, phase):
        g = self.g
        y, c, z, x = self.place
        t = self.target
        if phase == 0:
            return [(self.source, t.at[y, c, z, x], t.at[y, c, p, x], (y, c, p, x), z, p) for p in others(g.nz, z)]
        if phase == 3:
            return [(t.at[:, c], t.at[:, c], t.at[:, 1 - c], (y, 1 - c, z, x), c, 1 - c)]
        along_x = (phase == 1) == (self.colour == 0)
        if along_x:
            cut = (lambda p: t.at[y, c, :, p]) if phase == 1 else (lambda p: t.at[:, c, :, p])
            return [(cut(x), cut(x), cut(p), (y, c, z, p), x, p) for p in others(g.nx, x)]
        cut = (lambda p: t.at[p, c, :, x]) if phase == 1 else (lambda p: t.at[p, c])
        return [(cut(y), cut(y), cut(p), (p, c, z, x), y, p) for p in others(g.ny, y)]

    def go(self, phase, entry):
        src, dst, _, peer, mine, theirs = entry
        return pltpu.make_async_remote_copy(
            src_ref=src, dst_ref=dst, send_sem=self.send.at[phase, theirs], recv_sem=self.recv.at[phase, mine],
            device_id=self.g.device(*peer), device_id_type=MESH)

    def come(self, phase, entry):
        _, _, landed, peer, _, theirs = entry
        return pltpu.make_async_remote_copy(
            src_ref=landed, dst_ref=landed, send_sem=self.send.at[phase, theirs], recv_sem=self.recv.at[phase, theirs],
            device_id=self.g.device(*peer), device_id_type=MESH)

    def own(self):
        y, c, z, x = self.place
        return pltpu.make_async_copy(self.source, self.target.at[y, c, z, x], self.local)

    def start(self, phase):
        if phase == 0:
            self.own().start()
        for entry in self.plan(phase):
            self.go(phase, entry).start()

    def arrive(self, phase):
        if phase == 0:
            self.own().wait()
        for entry in self.plan(phase):
            self.come(phase, entry).wait_recv()

    def drain(self):
        for phase in range(4):
            for entry in self.plan(phase):
                self.go(phase, entry).wait_send()


def gather_kernel(grid, colours, *refs):
    n = len(colours)
    sources, targets, (send, recv, local) = refs[:n], refs[n : 2 * n], refs[2 * n :]
    place = grid.here()
    greet(grid, *place)
    jobs = [
        Gather(grid, place, sources[i], targets[i], colours[i], send.at[i], recv.at[i], local.at[i]) for i in range(n)
    ]
    for job in jobs:
        job.start(0)
    for tick in range(n + 2):
        for phase in (3, 2, 1):
            i = tick - (phase - 1)
            if 0 <= i < n:
                jobs[i].arrive(phase - 1)
                jobs[i].start(phase)
    for job in jobs:
        job.arrive(3)
    for job in jobs:
        job.drain()


def gather_all(grid, pieces, colours, collective_id):
    n = len(pieces)
    wide = max(grid.nx, grid.ny, grid.nz, 2)
    outs = pl.pallas_call(
        functools.partial(gather_kernel, grid, colours),
        out_shape=[jax.ShapeDtypeStruct(grid.blocks() + p.shape, p.dtype) for p in pieces],
        in_specs=[pl.BlockSpec(memory_space=pltpu.VMEM)] * n,
        out_specs=[pl.BlockSpec(memory_space=pl.ANY)] * n,
        scratch_shapes=[
            pltpu.SemaphoreType.DMA((n, 4, wide)),
            pltpu.SemaphoreType.DMA((n, 4, wide)),
            pltpu.SemaphoreType.DMA((n,)),
        ],
        compiler_params=pltpu.CompilerParams(collective_id=collective_id, has_side_effects=True),
        name="gather_parameters",
    )(*pieces)
    return outs


class Scatter:
    def __init__(self, grid, place, source, target, held, land, colour, send, recv, local):
        self.g, self.place, self.colour = grid, place, colour
        self.source, self.target, self.held, self.land = source, target, held, land
        self.send, self.recv, self.local = send, recv, local

    def along_y(self, phase):
        return (phase == 1) == (self.colour == 0)

    def plan(self, phase):
        g, held, land = self.g, self.held, self.land
        y, c, z, x = self.place
        if phase == 0:
            return [(self.source.at[:, 1 - c], lambda s: land[0], (y, 1 - c, z, x), c, 1 - c)]
        if phase == 3:
            return [(held.at[y, p, x], lambda s: land[3].at[s], (y, c, p, x), z, p) for p in others(g.nz, z)]
        if self.along_y(phase):
            cut = (lambda p: held.at[p]) if phase == 1 else (lambda p: held.at[p, :, x])
            return [(cut(p), lambda s: land[phase].at[s], (p, c, z, x), y, p) for p in others(g.ny, y)]
        cut = (lambda p: held.at[:, :, p]) if phase == 1 else (lambda p: held.at[y, :, p])
        return [(cut(p), lambda s: land[phase].at[s], (y, c, z, p), x, p) for p in others(g.nx, x)]

    def own(self):
        return pltpu.make_async_copy(self.source.at[:, self.place[1]], self.held, self.local)

    def go(self, phase, entry):
        src, spot, peer, mine, theirs = entry
        return pltpu.make_async_remote_copy(
            src_ref=src, dst_ref=spot(mine), send_sem=self.send.at[phase, theirs], recv_sem=self.recv.at[phase, mine],
            device_id=self.g.device(*peer), device_id_type=MESH)

    def come(self, phase, entry):
        src, spot, peer, mine, theirs = entry
        return pltpu.make_async_remote_copy(
            src_ref=spot(theirs), dst_ref=spot(theirs), send_sem=self.send.at[phase, theirs],
            recv_sem=self.recv.at[phase, theirs], device_id=self.g.device(*peer), device_id_type=MESH)

    def start(self, phase):
        if phase == 0:
            self.own().start()
        for entry in self.plan(phase):
            self.go(phase, entry).start()

    def finish(self, phase):
        g, held, land = self.g, self.held, self.land
        y, c, z, x = self.place
        if phase == 0:
            self.own().wait()
        plan = self.plan(phase)
        for entry in plan:
            self.come(phase, entry).wait_recv()
        kind = held.dtype
        f32 = jnp.float32

        def add(at, parts, out=None):
            total = held[at].astype(f32)
            for part in parts:
                total = total + part.astype(f32)
            if out is None:
                held[at] = total.astype(kind)
            else:
                out[...] = total

        slots = [entry[4] for entry in plan]
        if phase == 0:
            def body(i, carry):
                at = (i // (g.nz * g.nx), i // g.nx % g.nz, i % g.nx)
                add(at, [land[0][at]])
                return carry
            lax.fori_loop(0, g.ny * g.nz * g.nx, body, 0)
        elif phase == 3:
            add((y, z, x), [land[3][s] for s in slots], self.target)
        elif phase == 1 and self.along_y(1):
            def body(i, carry):
                add((y, i // g.nx, i % g.nx), [land[1][s, i // g.nx, i % g.nx] for s in slots])
                return carry
            lax.fori_loop(0, g.nz * g.nx, body, 0)
        elif phase == 1:
            def body(i, carry):
                add((i // g.nz, i % g.nz, x), [land[1][s, i // g.nz, i % g.nz] for s in slots])
                return carry
            lax.fori_loop(0, g.ny * g.nz, body, 0)
        else:
            def body(i, carry):
                add((y, i, x), [land[2][s, i] for s in slots])
                return carry
            lax.fori_loop(0, g.nz, body, 0)

    def drain(self):
        for phase in range(4):
            for entry in self.plan(phase):
                self.go(phase, entry).wait_send()


def scatter_scratch(grid, piece, kind, colour):
    ny, nz, nx = grid.ny, grid.nz, grid.nx
    if colour == 0:
        one, two = (ny, nz, nx), (nx, nz)
    else:
        one, two = (nx, ny, nz), (ny, nz)
    return [pltpu.VMEM(s + piece, kind) for s in ((ny, nz, nx), (ny, nz, nx), one, two, (nz,))]


def scatter_kernel(grid, colours, *refs):
    n = len(colours)
    sources, targets = refs[:n], refs[n : 2 * n]
    bufs = refs[2 * n : 7 * n]
    send, recv, local = refs[7 * n :]
    place = grid.here()
    greet(grid, *place)
    jobs = [
        Scatter(grid, place, sources[i], targets[i], bufs[5 * i], bufs[5 * i + 1 : 5 * i + 5], colours[i],
                send.at[i], recv.at[i], local.at[i])
        for i in range(n)
    ]
    for job in jobs:
        job.start(0)
    for tick in range(n + 2):
        for phase in (3, 2, 1):
            i = tick - (phase - 1)
            if 0 <= i < n:
                jobs[i].finish(phase - 1)
                jobs[i].start(phase)
    for job in jobs:
        job.finish(3)
    for job in jobs:
        job.drain()


def scatter_all(grid, arrays, colours, collective_id):
    n = len(arrays)
    wide = max(grid.nx, grid.ny, grid.nz, 2)
    scratch = []
    for a, colour in zip(arrays, colours):
        scratch += scatter_scratch(grid, a.shape[4:], a.dtype, colour)
    return pl.pallas_call(
        functools.partial(scatter_kernel, grid, colours),
        out_shape=[jax.ShapeDtypeStruct(a.shape[4:], jnp.float32) for a in arrays],
        in_specs=[pl.BlockSpec(memory_space=pl.ANY)] * n,
        out_specs=[pl.BlockSpec(memory_space=pltpu.VMEM)] * n,
        scratch_shapes=scratch + [
            pltpu.SemaphoreType.DMA((n, 4, wide)),
            pltpu.SemaphoreType.DMA((n, 4, wide)),
            pltpu.SemaphoreType.DMA((n,)),
        ],
        compiler_params=pltpu.CompilerParams(
            collective_id=collective_id, has_side_effects=True, vmem_limit_bytes=60000000),
        name="scatter_gradients",
    )(*arrays)


HD = 64
EPS = 1e-05
F32, BF16 = jnp.float32, jnp.bfloat16


def layer_norm(values, gain, shift):
    center = values - jnp.mean(values, axis=-1, keepdims=True)
    inverse = lax.rsqrt(jnp.mean(center * center, axis=-1, keepdims=True) + EPS)
    normed = center * inverse
    return normed * gain.astype(F32) + shift.astype(F32), normed, inverse


def norm_back(grad_out, gain, normed, inverse):
    scaled = grad_out * gain.astype(F32)
    grad_in = inverse * (
        scaled
        - jnp.mean(scaled, axis=-1, keepdims=True)
        - normed * jnp.mean(scaled * normed, axis=-1, keepdims=True)
    )
    return grad_in, jnp.sum(grad_out * normed, axis=0), jnp.sum(grad_out, axis=0)


def dot(left, right, dims=((1,), (0,))):
    return lax.dot_general(left, right, (dims, ((), ())), preferred_element_type=F32)


def rows_of(left, right):
    return dot(left, right, ((0,), (0,)))


def flipped(left, right):
    return dot(left, right, ((1,), (1,)))


def gelu_slope(values):
    cumulative = 0.5 * (1.0 + lax.erf(values * 0.7071067811865476))
    return cumulative + values * jnp.exp(-0.5 * values * values) * 0.3989422804014327


def row_mask(ids):
    length = ids.shape[0]
    places = lax.broadcasted_iota(jnp.int32, (length, length), 0)
    others_ = lax.broadcasted_iota(jnp.int32, (length, length), 1)
    return (ids[:, None] == ids[None, :]) & (ids[None, :] >= 0) | (places == others_)


def row_scores(query, keys, ids):
    scores = jnp.einsum("qhd,khd->hqk", query, keys, preferred_element_type=F32) * HD ** -0.5
    return jnp.where(row_mask(ids)[None], scores, -1e30)


def attend_row(query, keys, values, ids):
    scores = row_scores(query, keys, ids)
    peak = jnp.max(scores, axis=-1, keepdims=True)
    log_total = peak + jnp.log(jnp.sum(jnp.exp(scores - peak), axis=-1, keepdims=True))
    probs = jnp.exp(scores - log_total).astype(BF16)
    return jnp.einsum("hqk,khd->qhd", probs, values, preferred_element_type=F32), log_total


def attend_back(query, keys, values, grad_mixed, ids, log_total):
    probs = jnp.exp(row_scores(query, keys, ids) - log_total)
    grad_values = jnp.einsum("hqk,qhd->khd", probs.astype(BF16), grad_mixed, preferred_element_type=F32)
    grad_probs = jnp.einsum("qhd,khd->hqk", grad_mixed, values, preferred_element_type=F32)
    grad_low = (probs * (grad_probs - jnp.sum(probs * grad_probs, axis=-1, keepdims=True))).astype(BF16)
    scale = HD ** -0.5
    grad_query = jnp.einsum("hqk,khd->qhd", grad_low, keys, preferred_element_type=F32) * scale
    grad_keys = jnp.einsum("hqk,qhd->khd", grad_low, query, preferred_element_type=F32) * scale
    return grad_query.astype(BF16), grad_keys.astype(BF16), grad_values.astype(BF16)


MATRICES = ("wq", "wk", "wv", "wo", "wu", "wd")
COLOURS = (0, 1, 1, 0, 0, 1)
VECTORS = (
    "g1", "s1", "bq", "bv", "g2", "s2", "bo",
    "g3", "s3", "bd", "bu", "g4", "s4",
)
ORDER = (
    "g1", "s1", "wq", "bq", "wk", "wv", "bv",
    "g2", "s2", "wo", "bo", "g3", "s3", "wu",
    "bu", "g4", "s4", "wd", "bd",
)


def pack(vectors):
    flat = jnp.concatenate(vectors, axis=-1)
    size = flat.shape[-1]
    padded = -(-size // 1024) * 1024
    flat = jnp.pad(flat, [(0, 0)] * (flat.ndim - 1) + [(0, padded - size)])
    return flat.reshape(flat.shape[:-1] + (padded // 128, 128))


def fetch(grid, own):
    pieces = [own[name] for name in MATRICES] + [pack([own[name] for name in VECTORS])]
    found = gather_all(grid, pieces, COLOURS + (0,), 0)
    full = {name: got.reshape(-1, got.shape[-1]) for name, got in zip(MATRICES, found)}
    small = found[-1].reshape(-1, pieces[-1].size)
    at = 0
    for name in VECTORS:
        size = own[name].shape[0]
        full[name] = small[:, at : at + size].reshape(-1)
        at += size
    return full


def hand_out(grid, grads, own):
    blocks = grid.blocks()
    count = grid.ny * 2 * grid.nz * grid.nx
    arrays = [grads[name].reshape(blocks + own[name].shape) for name in MATRICES]
    small = pack([grads[name].reshape(count, -1) for name in VECTORS])
    arrays.append(small.reshape(blocks + small.shape[1:]))
    owned = scatter_all(grid, arrays, COLOURS + (0,), 1)
    out = dict(zip(MATRICES, owned))
    small = owned[-1].reshape(-1)
    at = 0
    for name in VECTORS:
        size = own[name].shape[0]
        out[name] = small[at : at + size]
        at += size
    return out


def on_device(grid, inputs, doc_ids, *rest):
    own = dict(zip(ORDER, rest[:-1]))
    cotangent = rest[-1]
    batches, rows, length, width = inputs.shape
    flat = inputs.reshape(-1, width).astype(F32)
    ids = doc_ids.reshape(-1, length)
    p = fetch(grid, own)
    heads = (-1, length, width // HD, HD)

    normed_in, n1, r1 = layer_norm(flat, p["g1"], p["s1"])
    a = normed_in.astype(BF16)
    q = (dot(a, p["wq"]) + p["bq"].astype(F32)).astype(BF16).reshape(heads)
    k = dot(a, p["wk"]).astype(BF16).reshape(heads)
    v = (dot(a, p["wv"]) + p["bv"].astype(F32)).astype(BF16).reshape(heads)
    mixed, totals = [], []
    for i in range(q.shape[0]):
        o, t = attend_row(q[i], k[i], v[i], ids[i])
        mixed.append(o.reshape(length, width))
        totals.append(t)
    o = jnp.concatenate(mixed)
    normed_mid, n2, r2 = layer_norm(o, p["g2"], p["s2"])
    b = normed_mid.astype(BF16)
    x1 = flat + dot(b, p["wo"]) + p["bo"].astype(F32)
    normed_feed, n3, r3 = layer_norm(x1, p["g3"], p["s3"])
    c = normed_feed.astype(BF16)
    u = dot(c, p["wu"]) + p["bu"].astype(F32)
    normed_act, n4, r4 = layer_norm(jax.nn.gelu(u, approximate=False), p["g4"], p["s4"])
    e = normed_act.astype(BF16)
    out = (x1 + dot(e, p["wd"]) + p["bd"].astype(F32)).astype(BF16)

    g = {}
    gd = cotangent.reshape(-1, width)
    gy = gd.astype(F32)
    g["wd"] = rows_of(e, gd).astype(BF16)
    g["bd"] = jnp.sum(gy, axis=0)
    gg, g["g4"], g["s4"] = norm_back(flipped(gd, p["wd"]), p["g4"], n4, r4)
    gu = (gg * gelu_slope(u)).astype(BF16)
    g["wu"] = rows_of(c, gu).astype(BF16)
    g["bu"] = jnp.sum(gu.astype(F32), axis=0)
    gf, g["g3"], g["s3"] = norm_back(flipped(gu, p["wu"]), p["g3"], n3, r3)
    gx1 = gy + gf
    gh = gx1.astype(BF16)
    g["wo"] = rows_of(b, gh).astype(BF16)
    g["bo"] = jnp.sum(gh.astype(F32), axis=0)
    gof, g["g2"], g["s2"] = norm_back(flipped(gh, p["wo"]), p["g2"], n2, r2)
    go = gof.astype(BF16).reshape(heads)
    parts = [attend_back(q[i], k[i], v[i], go[i], ids[i], totals[i]) for i in range(q.shape[0])]
    gq, gk, gv = (jnp.concatenate([part[j].reshape(length, width) for part in parts]) for j in range(3))
    g["wq"] = rows_of(a, gq).astype(BF16)
    g["bq"] = jnp.sum(gq.astype(F32), axis=0)
    g["wk"] = rows_of(a, gk).astype(BF16)
    g["wv"] = rows_of(a, gv).astype(BF16)
    g["bv"] = jnp.sum(gv.astype(F32), axis=0)
    ga = flipped(gq, p["wq"]) + flipped(gk, p["wk"]) + flipped(gv, p["wv"])
    gf1, g["g1"], g["s1"] = norm_back(ga, p["g1"], n1, r1)
    input_grad = (gx1 + gf1).astype(BF16)
    got = hand_out(grid, g, own)
    return (out.reshape(inputs.shape), input_grad.reshape(inputs.shape)) + tuple(got[name] for name in ORDER)


def solution(mesh):
    both = ("dp", "shard")
    grid = Grid(mesh.shape["dp"], mesh.shape["shard"])
    rows = P(None, both, None, None)
    params = tuple(P(both, None) if name in MATRICES else P(both) for name in ORDER)
    return jax.shard_map(
        functools.partial(on_device, grid),
        mesh=mesh,
        in_specs=(rows, P(None, both, None)) + params + (rows,),
        out_specs=(rows, rows) + params,
        check_vma=False,
    )
```

time: 2300 us -> 546 us (0.24)
  waiting for transfers between devices: 1750 us -> 0 us
  Pallas kernels: 0 us -> 254 us
  matrix products: 270 us -> 174 us
  blocking collectives: 84.6 us -> 0 us
  local copies, waits for them, and re-layouts: 78.1 us -> 42 us
  other arithmetic: 89.3 us -> 64.4 us
    all_gather x24 -> x0, waiting for transfers between devices: 909 us -> none  [the longest x4 191 us: fetch_mixer(): lax.all_gather(key_weight, ('dp', 'shard'), axis=0, tiled=True)]
    reduce_scatter x6 -> x0, waiting for transfers between devices: 691 us -> none  [the longest x1 142 us: on_device(): lax.psum_scatter(feed_three, ('dp', 'shard'), scatter_dimension=0, tiled=...]
    pallas_call x0 -> x2, Pallas kernels: none -> 254 us  [the longest x1 135 us: scatter_all(): pl.pallas_call(functools.partial(scatter_kernel, grid, colours), out_shap...]
    unnamed x32 -> x0, waiting for transfers between devices: 154 us -> none
    dot_general x50 -> x30, matrix products: 270 us -> 174 us  [the longest x18 120 us: dot(): lax.dot_general(left, right, (dims, ((), ())), preferred_element_type=F32)]
    unnamed x2 -> x0, blocking collectives: 84.6 us -> none
    unnamed x265 -> x193, local copies, waits for them, and re-layouts: 51.2 us -> 21.2 us
  transfers between devices with their start and end apart: 31 -> 0, of which waited for: 28 -> 0; matrix products, arithmetic and copies ran while one was open for 18% -> 0% of each run, Pallas kernels for 0% -> 0%
where the time goes in v1:
time: 546 us; the launch traced here: 537 us
  Pallas kernels  254 us (47%)
  matrix products  174 us (32%)
  other arithmetic  64.4 us (12%)
  local copies, waits for them, and re-layouts  42 us (8%)
    pallas_call x1, Pallas kernels, scatter_all(): pl.pallas_call(functools.partial(scatter_kernel, grid, colours), out_shap...  135 us
    dot_general x18, matrix products, dot(): lax.dot_general(left, right, (dims, ((), ())), preferred_element_type=F32)  120 us
    pallas_call x1, Pallas kernels, gather_all(): pl.pallas_call(functools.partial(gather_kernel, grid, colours), out_shape...  119 us
    unnamed x193, local copies, waits for them, and re-layouts  21.2 us
    dot_general x2, matrix products, attend_back(): jnp.einsum('qhd,khd->hqk', grad_mixed, values, preferred_element_type=F32)  20.5 us
    reduce_sum x1, other arithmetic, on_device(): g['bu'] = jnp.sum(gu.astype(F32), axis=0)  19.1 us
    convert_element_type x2, other arithmetic, attend_back(): (probs * (grad_probs - jnp.sum(probs * grad_probs, axis=-1, keepdims=True...  16.9 us

profile of v1, /device:TPU:0, one launch (start us, length us, event | category | flops | bytes accessed | tf_op | source)
XLA Modules:
  0.0 537.2 jit_solution(16054953579317976804)
XLA Ops:
  0.7 8.9 %concatenate.18 = bf16[528]{0:T(1024)(128)(2,1)S(1)} concatenate(bf16[24]{0:T(256)(128)(2,1)} %param.24, bf16[24]{0:T(256)(128)(2,1)} %param.25, bf16[24]{0:T(256)(128)(2,1)} %param.27, bf16[24]{0:T(256)(128)(2,1)} %param.30, bf16[24]{0:T(256)(128)(2,1)} %param.31, bf16[24]{0:T(256)(128)(2,1)} %param.32, bf16[24]{0:T(256)(128)(2,1)} %param.34, bf16[24]{0:T(256)(128)(2,1)} %param.35, ...), dimensions={0} | concatenate | bytes 2112 | tf_op jit(solution)/shard_map/concatenate | solution.py:380
  10.1 119.0 %gather_parameters.1 = (bf16[2,2,4,2,24,768]{5,4,3,2,1,0:T(8,128)(2,1)}, bf16[2,2,4,2,24,768]{5,4,3,2,1,0:T(8,128)(2,1)}, bf16[2,2,4,2,24,768]{5,4,3,2,1,0:T(8,1...) custom-call(bf16[24,768]{1,0:T(8,128)(2,1)} %refs_0_.1, ...), custom_call_target="tpu_custom_call" | custom-call | tf_op jit(solution)/shard_map/gather_parameters/pallas_call | solution.py:129
  155.1 6.5 %fusion.50 = f32[12,64,512]{2,1,0:T(8,128)S(1)} fusion(bf16[512,12,64]{0,2,1:T(8,128)(2,1)S(1)} %bitcast.201, f32[12,512,512]{1,2,0:T(8,128)} %copy-done, f32[12,512]{1,0:T(8,128)S(1)} %log_add_fusion.1, pred[512,512]{0,1:T(8,128)(4,1)S(1)} %fusion.42), kind=kOutput, calls=%fused_computation.123 | convolution fusion | flops 415236096 | bytes 15228928 | tf_op jit(solution)/shard_map/hqk,khd->qhd/dot_general | solution.py:352
  168.5 4.3 fusion.47
  174.3 3.7 fusion.82
  180.7 37.3 %fusion.73 = (f32[1024]{0:T(1024)S(1)}, f32[1024,3072]{1,0:T(8,128)S(1)}, f32[1024,3072]{1,0:T(8,128)}) fusion(f32[3072]{0:T(1024)S(1)} %reshape.664, bf16[768,3072]{1,0:T(8,128)(2,1)} %bitcast.241, f32[1024,768]{1,0:T(8,128)} %copy-done.13, f32[768]{0:T(1024)S(1)} %reshape.663, f32[768]{0:T(1024)S(1)} %reshape.662, f32[1024]{0:T(1024)S(1)} %add_rsqrt_fusion.1, ...), kind=kOutput, calls=%fused_computation.176 | convolution fusion | flops 5043387392 | bytes 33060864 | tf_op jit(solution)/shard_map/dot_general | solution.py:319
  219.3 3.3 copy-done.5
  222.8 13.4 %fusion.8 = (f32[3072]{0:T(1024)S(1)}, f32[1024]{0:T(1024)S(1)}, f32[1024]{0:T(1024)S(1)}, f32[3072,1024]{0,1:T(8,128)}) fusion(f32[1024,3072]{1,0:T(8,128)} %copy-done.5, f32[1024]{0:T(1024)S(1)} %add_rsqrt_fusion, f32[1024]{0:T(1024)S(1)} %broadcast_multiply_fusion.2, f32[3072]{0:T(1024)S(1)} %reshape.665, bf16[3072,768]{1,0:T(8,128)(2,1)} %bitcast.239, ...), kind=kOutput, calls=%fused_computation.12 | convolution fusion | flops 4856998912 | bytes 31498240 | tf_op jit(solution)/shard_map/dot_general | solution.py:319
  236.2 19.1 %convert_reduce_fusion = (f32[3072]{0:T(1024)S(1)}, bf16[1024,3072]{1,0:T(8,128)(2,1)S(1)}, bf16[1024,3072]{1,0:T(8,128)(2,1)}) fusion(f32[1024,3072]{1,0:T(8,128)} %get-tuple-element.160, f32[3072]{0:T(1024)S(1)} %reshape.664, f32[1024]{0:T(1024)S(1)} %get-tuple-element.169, f32[1024,3072]{1,0:T(8,128)} %copy-done.5, f32[1024]{0:T(1024)S(1)} %broadcast_multiply_fusion.2, ...), kind=kLoop, calls=%fused_computation.13 | loop fusion | flops 72348672 | bytes 50397184 | tf_op jit(solution)/shard_map/reduce_sum | solution.py:455
  255.4 10.3 %multiply_reduce_fusion.4 = (f32[768]{0:T(1024)S(1)}, f32[1024]{0:T(1024)S(1)}, f32[1024]{0:T(1024)S(1)}, f32[768]{0:T(1024)S(1)}, f32[1024,768]{1,0:T(8,128)S(1)}) fusion(f32[1024,768]{1,0:T(8,128)S(1)} %copy-done.14, f32[1024]{0:T(1024)S(1)} %add_rsqrt_fusion.1, f32[1024]{0:T(1024)S(1)} %broadcast_multiply_fusion.9, f32[768]{0:T(1024)S(1)} %reshape.662, ...), kind=kOutput, calls=%fused_computation.76 | convolution fusion | flops 4838912000 | bytes 17327104 | tf_op jit(solution)/shard_map/dot_general | solution.py:319
  274.0 5.8 %convolution_convert_fusion.8 = bf16[12,64,512]{2,1,0:T(8,128)(2,1)} fusion(bf16[512,12,64]{0,2,1:T(8,128)(2,1)} %bitcast.205, f32[12,512,512]{1,2,0:T(8,128)S(1)} %bitcast.162, f32[12,512]{1,0:T(8,128)S(1)} %copy-done.48, pred[512,512]{0,1:T(8,128)(4,1)S(1)} %copy-done.26), kind=kOutput, calls=%fused_computation.111 | convolution fusion | flops 415629312 | bytes 14442496 | tf_op jit(solution)/shard_map/hqk,qhd->khd/dot_general | solution.py:357
  279.8 4.3 convolution_convert_fusion.7
  285.3 13.5 %multiply_reduce_fusion.1 = (f32[12,512]{1,0:T(8,128)S(1)}, f32[12,512,512]{1,2,0:T(8,128)}) fusion(f32[12,512,512]{1,2,0:T(8,128)} %copy-done, f32[12,512]{1,0:T(8,128)S(1)} %copy-done.48, pred[512,512]{0,1:T(8,128)(4,1)S(1)} %copy-done.26, bf16[512,12,64]{0,2,1:T(8,128)(2,1)} %bitcast.206, bf16[512,12,64]{0,2,1:T(8,128)(2,1)} %bitcast.202), kind=kOutput, calls=%fused_computation.17 | convolution fusion | flops 418375680 | bytes 27049984 | tf_op jit(solution)/shard_map/qhd,khd->hqk/dot_general | solution.py:358
  298.9 9.9 %multiply_convert_fusion.1 = bf16[12,512,512]{1,2,0:T(8,128)(2,1)S(1)} fusion(f32[12,512,512]{1,2,0:T(8,128)} %get-tuple-element.167, f32[12,512,512]{1,2,0:T(8,128)} %copy-done, f32[12,512]{1,0:T(8,128)S(1)} %get-tuple-element.166, f32[12,512]{1,0:T(8,128)S(1)} %copy-done.48, pred[512,512]{0,1:T(8,128)(4,1)S(1)} %copy-done.26), kind=kLoop, calls=%fused_computation.16 | loop fusion | flops 18874368 | bytes 31768576 | tf_op jit(solution)/shard_map/convert_element_type | solution.py:359
  311.6 7.0 %multiply_reduce_fusion = (f32[12,512]{1,0:T(8,128)S(1)}, f32[12,512,512]{1,2,0:T(8,128)}) fusion(f32[12,512,512]{1,2,0:T(8,128)S(1)} %bitcast.166, f32[12,512]{1,0:T(8,128)S(1)} %copy-done.50, pred[512,512]{0,1:T(8,128)(4,1)S(1)} %copy-done.28, bf16[512,12,64]{0,2,1:T(8,128)(2,1)S(1)} %bitcast.204, bf16[512,12,64]{0,2,1:T(8,128)(2,1)S(1)} %bitcast.200), kind=kOutput, calls=%fused_computation.15 | convolution fusion | flops 418375680 | bytes 27049984 | tf_op jit(solution)/shard_map/qhd,khd->hqk/dot_general | solution.py:358
  318.6 7.0 %multiply_convert_fusion = bf16[12,512,512]{1,2,0:T(8,128)(2,1)S(1)} fusion(f32[12,512,512]{1,2,0:T(8,128)} %get-tuple-element.165, f32[12,512,512]{1,2,0:T(8,128)S(1)} %bitcast.166, f32[12,512]{1,0:T(8,128)S(1)} %get-tuple-element.164, f32[12,512]{1,0:T(8,128)S(1)} %copy-done.50, pred[512,512]{0,1:T(8,128)(4,1)S(1)} %copy-done.28), kind=kLoop, calls=%fused_computation.14 | loop fusion | flops 18874368 | bytes 31768576 | tf_op jit(solution)/shard_map/convert_element_type | solution.py:359
  328.6 4.9 multiply_convert_fusion.4
  339.4 4.9 fusion.40
  345.0 5.2 reduce_sum.329
  353.0 10.6 %convolution_convert_fusion.1 = bf16[768,3072]{1,0:T(8,128)(2,1)} fusion(bf16[1024,3072]{1,0:T(8,128)(2,1)} %copy-done.29, f32[1024,768]{1,0:T(8,128)} %copy-done.13, f32[768]{0:T(1024)S(1)} %reshape.663, f32[768]{0:T(1024)S(1)} %reshape.662, f32[1024]{0:T(1024)S(1)} %add_rsqrt_fusion.1, f32[1024]{0:T(1024)S(1)} %broadcast_multiply_fusion.9), kind=kOutput, calls=%fused_computation.49 | convolution fusion | flops 4838129664 | bytes 14170112 | tf_op jit(solution)/shard_map/dot_general | solution.py:319
  373.7 7.2 %convolution_convert_fusion = bf16[3072,768]{1,0:T(8,128)(2,1)} fusion(bf16[1024,3072]{1,0:T(8,128)(2,1)S(1)} %bitcast.194, bf16[1024,768]{1,0:T(8,128)(2,1)S(1)} %bitcast.196), kind=kOutput, calls=%fused_computation.48 | convolution fusion | flops 4834197504 | bytes 12582912 | tf_op jit(solution)/shard_map/dot_general | solution.py:319
  380.9 135.2 %scatter_gradients.1 = (f32[24,768]{1,0:T(8,128)}, f32[24,768]{1,0:T(8,128)}, f32[24,768]{1,0:T(8,128)}, f32[24,768]{1,0:T(8,128)}, f32[24,3072]{1,0:T(8,128)}, /*index=5*/f32[96,768]{1,0:T(8,128)}, f32[8,128]{1,0:T(8,128)}) custom-call(bf16[2,2,4,2,24,768]{5,4,3,2,1,0:T(8,128)(2,1)} %bitcast.214, bf16[2,2,4,2,24,768]{5,4,3,2,1,0:T(8,128)(2,1)} %bitcast.213, ...), custom_call_target="tpu_custom_call" | custom-call | tf_op jit(solution)/shard_map/scatter_gradients/pallas_call | solution.py:280
  519.2 3.5 fusion.37
  522.9 10.0 %add_convert_fusion.1 = bf16[1024,768]{1,0:T(8,128)(2,1)} fusion(f32[1024,768]{1,0:T(8,128)} %copy-done.13, bf16[1024,3072]{1,0:T(8,128)(2,1)} %get-tuple-element.112, bf16[3072,768]{1,0:T(8,128)(2,1)} %bitcast.240, f32[768]{0:T(1024)S(1)} %reshape.667), kind=kOutput, calls=%fused_computation.86 | convolution fusion | flops 4834197504 | bytes 15731712 | tf_op jit(solution)/shard_map/dot_general | solution.py:319
  (283 shorter events, 80.1 us)
Async XLA Ops:
  0.7 132.5 %copy-start.6 = (bf16[2,1,512,768]{3,2,1,0:T(8,128)(2,1)S(1)}, bf16[2,1,512,768]{3,2,1,0:T(8,128)(2,1)}, u32[]{:S(2)}) copy-start(bf16[2,1,512,768]{3,2,1,0:T(8,128)(2,1)} %param.22) | copy-start | bytes 4718596
  142.7 12.4 %copy-start.25 = (pred[512,512]{0,1:T(8,128)(4,1)}, pred[512,512]{0,1:T(8,128)(4,1)S(1)}, u32[]{:S(2)}) copy-start(pred[512,512]{0,1:T(8,128)(4,1)S(1)} %fusion.42) | copy-start | bytes 786436
  161.6 108.1 %copy-start.8 = (f32[12,64,512]{2,1,0:T(8,128)}, f32[12,64,512]{2,1,0:T(8,128)S(1)}, u32[]{:S(2)}) copy-start(f32[12,64,512]{2,1,0:T(8,128)S(1)} %fusion.50) | copy-start | bytes 4718596
  173.2 94.4 %copy-start.58 = (f32[1024]{0:T(1024)}, f32[1024]{0:T(1024)S(1)}, u32[]{:S(2)}) copy-start(f32[1024]{0:T(1024)S(1)} %broadcast_multiply_fusion.10) | copy-start | bytes 12292
  174.0 93.5 %copy-start.65 = (f32[1024]{0:T(1024)}, f32[1024]{0:T(1024)S(1)}, u32[]{:S(2)}) copy-start(f32[1024]{0:T(1024)S(1)} %add_rsqrt_fusion.2) | copy-start | bytes 12292
  174.1 93.4 %copy-start.63 = (f32[768]{0:T(1024)}, f32[768]{0:T(1024)S(1)}, u32[]{:S(2)}) copy-start(f32[768]{0:T(1024)S(1)} %reshape.659) | copy-start | bytes 9220
  236.2 19.1 %copy-start.14 = (f32[1024,768]{1,0:T(8,128)S(1)}, f32[1024,768]{1,0:T(8,128)}, u32[]{:S(2)}) copy-start(f32[1024,768]{1,0:T(8,128)} %copy-done.13) | copy-start | bytes 9437188
  255.3 10.3 %copy-start.29 = (bf16[1024,3072]{1,0:T(8,128)(2,1)}, bf16[1024,3072]{1,0:T(8,128)(2,1)S(1)}, u32[]{:S(2)}) copy-start(bf16[1024,3072]{1,0:T(8,128)(2,1)S(1)} %get-tuple-element.107) | copy-start | bytes 18874372
  285.3 26.2 %slice-start.6 = ((s8[12582912]{0:T(1024)(128)(4,1)}), s8[4194304]{0:T(1024)(128)(4,1)S(1)}, s32[]{:S(2)}) async-start(s8[12582912]{0:T(1024)(128)(4,1)} %bitcast.165), calls=%async_computation.6 | async-start | bytes 8388608
  285.3 26.2 %slice-start.7 = ((s8[12582912]{0:T(1024)(128)(4,1)}), s8[4194304]{0:T(1024)(128)(4,1)S(1)}, s32[]{:S(2)}) async-start(s8[12582912]{0:T(1024)(128)(4,1)} %bitcast.165), calls=%async_computation.7 | async-start | bytes 8388608
  298.9 12.7 %slice-start.8 = ((s8[12582912]{0:T(1024)(128)(4,1)}), s8[4194304]{0:T(1024)(128)(4,1)S(1)}, s32[]{:S(2)}) async-start(s8[12582912]{0:T(1024)(128)(4,1)} %bitcast.165), calls=%async_computation.8 | async-start | bytes 8388608
  353.0 10.6 %copy-start.9 = (f32[12,64,512]{2,1,0:T(8,128)S(1)}, f32[12,64,512]{2,1,0:T(8,128)}, u32[]{:S(2)}) copy-start(f32[12,64,512]{2,1,0:T(8,128)} %copy-done.8) | copy-start | bytes 4718596
  353.0 10.6 %copy-start.12 = (f32[12,64,512]{2,1,0:T(8,128)S(1)}, f32[12,64,512]{2,1,0:T(8,128)}, u32[]{:S(2)}) copy-start(f32[12,64,512]{2,1,0:T(8,128)} %copy-done.10) | copy-start | bytes 4718596
  353.0 10.6 %copy-start.16 = (f32[1024,768]{1,0:T(8,128)S(1)}, f32[1024,768]{1,0:T(8,128)}, u32[]{:S(2)}) copy-start(f32[1024,768]{1,0:T(8,128)} %copy-done.15) | copy-start | bytes 9437188
  353.0 10.6 %copy-start.59 = (f32[1024]{0:T(1024)S(1)}, f32[1024]{0:T(1024)}, u32[]{:S(2)}) copy-start(f32[1024]{0:T(1024)} %copy-done.58) | copy-start | bytes 12292
  353.0 10.6 %copy-start.64 = (f32[768]{0:T(1024)S(1)}, f32[768]{0:T(1024)}, u32[]{:S(2)}) copy-start(f32[768]{0:T(1024)} %copy-done.63) | copy-start | bytes 9220
  353.0 10.6 %copy-start.66 = (f32[1024]{0:T(1024)S(1)}, f32[1024]{0:T(1024)}, u32[]{:S(2)}) copy-start(f32[1024]{0:T(1024)} %copy-done.65) | copy-start | bytes 12292
  353.0 10.6 %copy-start.72 = (f32[768]{0:T(1024)S(1)}, f32[768]{0:T(1024)}, u32[]{:S(2)}) copy-start(f32[768]{0:T(1024)} %copy-done.71) | copy-start | bytes 9220
  522.8 10.0 %copy-start.54 = (f32[24,768]{1,0:T(8,128)S(1)}, f32[24,768]{1,0:T(8,128)}, u32[]{:S(2)}) copy-start(f32[24,768]{1,0:T(8,128)} %get-tuple-element.196) | copy-start | bytes 221188
  522.8 10.6 %copy-start.53 = (f32[24,768]{1,0:T(8,128)S(1)}, f32[24,768]{1,0:T(8,128)}, u32[]{:S(2)}) copy-start(f32[24,768]{1,0:T(8,128)} %get-tuple-element.198) | copy-start | bytes 221188
  522.8 11.3 %copy-start.52 = (f32[24,768]{1,0:T(8,128)S(1)}, f32[24,768]{1,0:T(8,128)}, u32[]{:S(2)}) copy-start(f32[24,768]{1,0:T(8,128)} %get-tuple-element.199) | copy-start | bytes 221188
  522.8 11.9 %copy-start.51 = (f32[24,768]{1,0:T(8,128)S(1)}, f32[24,768]{1,0:T(8,128)}, u32[]{:S(2)}) copy-start(f32[24,768]{1,0:T(8,128)} %get-tuple-element.203) | copy-start | bytes 221188
  522.8 12.5 %copy-start.46 = (f32[24,3072]{1,0:T(8,128)S(1)}, f32[24,3072]{1,0:T(8,128)}, u32[]{:S(2)}) copy-start(f32[24,3072]{1,0:T(8,128)} %get-tuple-element.207) | copy-start | bytes 884740
  522.9 13.2 %copy-start.45 = (f32[96,768]{1,0:T(8,128)S(1)}, f32[96,768]{1,0:T(8,128)}, u32[]{:S(2)}) copy-start(f32[96,768]{1,0:T(8,128)} %get-tuple-element.211) | copy-start | bytes 884740
  (67 other events, 245.1 us)

commit v2 on v1

v2 whole, which is shorter than its diff:
```python
import functools

import jax
import jax.numpy as jnp
from jax import lax
from jax.experimental import pallas as pl
from jax.experimental.pallas import tpu as pltpu
from jax.sharding import PartitionSpec as P


EPS = 1e-05
F32, BF16 = jnp.float32, jnp.bfloat16


def dot(left, right, dims=((1,), (0,))):
    return lax.dot_general(left, right, (dims, ((), ())), preferred_element_type=F32)


def flipped(left, right):
    return dot(left, right, ((1,), (1,)))


def eights(values):
    return jnp.sum(values.reshape(values.shape[0] // 8, 8, values.shape[1]), axis=0)


def mean_of(values):
    return jnp.sum(values, axis=-1, keepdims=True) * (1.0 / values.shape[-1])


def normed_of(values):
    center = values - mean_of(values)
    inverse = lax.rsqrt(mean_of(center * center) + EPS)
    return center * inverse, inverse


def feed_kernel(
    tile, chunk, tiles, x1_ref, gd_ref, wu_ref, wd_ref, g3_ref, s3_ref, bd_ref, bu_ref, g4_ref, s4_ref,
    out_ref, gx1_ref, dwu_ref, dwd_ref, d3_ref, dbu_ref, d4_ref,
    act, slope, scaled, turned, below, turned_c, kept_gd, acc, wide_acc, narrow_acc,
):
    step = pl.program_id(0)
    ff = bu_ref.shape[1]
    chunks = ff // chunk

    @pl.when(step == 0)
    def _():
        wide_acc[...] = jnp.zeros_like(wide_acc)
        narrow_acc[...] = jnp.zeros_like(narrow_acc)

    @pl.when(step < tiles)
    def _():
        rows = pl.ds(pl.multiple_of(step * tile, tile), tile)
        x1 = x1_ref[...]
        gd = gd_ref[...]
        gy = gd.astype(F32)
        kept_gd[rows, :] = gd
        n3, r3 = normed_of(x1)
        c = (n3 * g3_ref[...] + s3_ref[...]).astype(BF16)
        turned_c[:, rows] = c.T

        total = jnp.zeros((tile, 1), F32)
        for j in range(chunks):
            cols = slice(j * chunk, (j + 1) * chunk)
            u = dot(c, wu_ref[:, cols]) + bu_ref[:, cols]
            phi = 0.5 + 0.5 * lax.erf(u * 0.7071067811865476)
            g = u * phi
            act[:, cols] = g
            slope[:, cols] = phi + u * (jnp.exp(u * u * -0.5) * 0.3989422804014327)
            total += jnp.sum(g, axis=-1, keepdims=True)
        mean = total * (1.0 / ff)
        total = jnp.zeros((tile, 1), F32)
        for j in range(chunks):
            d = act[:, j * chunk : (j + 1) * chunk] - mean
            total += jnp.sum(d * d, axis=-1, keepdims=True)
        r4 = lax.rsqrt(total * (1.0 / ff) + EPS)

        sum_t = jnp.zeros((tile, 1), F32)
        sum_tn = jnp.zeros((tile, 1), F32)
        acc[...] = x1 + bd_ref[...]
        for j in range(chunks):
            cols = slice(j * chunk, (j + 1) * chunk)
            gain = g4_ref[:, cols]
            n = (act[:, cols] - mean) * r4
            act[:, cols] = n
            e = (n * gain + s4_ref[:, cols]).astype(BF16)
            turned[cols, rows] = e.T
            acc[...] += dot(e, wd_ref[cols, :])
            ge = flipped(gd, wd_ref[cols, :])
            wide_acc[0:8, cols] += eights(ge * n)
            wide_acc[8:16, cols] += eights(ge)
            t = ge * gain
            scaled[:, cols] = t
            sum_t += jnp.sum(t, axis=-1, keepdims=True)
            sum_tn += jnp.sum(t * n, axis=-1, keepdims=True)
        out_ref[...] = acc[...].astype(BF16)
        mean_t = sum_t * (1.0 / ff)
        mean_tn = sum_tn * (1.0 / ff)
        gc = jnp.zeros_like(x1)
        for j in range(chunks):
            cols = slice(j * chunk, (j + 1) * chunk)
            gg = r4 * (scaled[:, cols] - mean_t - act[:, cols] * mean_tn)
            gu = (gg * slope[:, cols]).astype(BF16)
            below[rows, cols] = gu
            wide_acc[16:24, cols] += eights(gu.astype(F32))
            gc += flipped(gu, wu_ref[:, cols])
        narrow_acc[0:8, :] += eights(gc * n3)
        narrow_acc[8:16, :] += eights(gc)
        narrow_acc[16:24, :] += eights(gy)
        t = gc * g3_ref[...]
        gx1_ref[...] = gy + r3 * (t - mean_of(t) - n3 * mean_of(t * n3))

    @pl.when(step >= tiles)
    def _():
        at = pl.multiple_of((step - tiles) * chunk, chunk)
        dwd_ref[...] = dot(turned[pl.ds(at, chunk), :], kept_gd[...]).astype(BF16)
        dwu_ref[...] = dot(turned_c[...], below[:, pl.ds(at, chunk)]).astype(BF16)

    @pl.when(step == tiles)
    def _():
        d3_ref[...] = jnp.sum(narrow_acc[...].reshape(3, 8, -1), axis=1)
        wide = jnp.sum(wide_acc[...].reshape(3, 8, -1), axis=1)
        d4_ref[...] = wide[0:2]
        dbu_ref[...] = wide[2:3]


def feed(x1, gd, wu, wd, g3, s3, bd, bu, g4, s4, tile=256, chunk=512):
    tokens, width = x1.shape
    ff = wu.shape[1]
    tiles, chunks = tokens // tile, ff // chunk
    row = pl.BlockSpec((tile, width), lambda i: (jnp.minimum(i, tiles - 1), 0))
    whole = lambda a: pl.BlockSpec(a.shape, lambda i: (0, 0), pipeline_mode=pl.Buffered(1))
    late = lambda i: jnp.maximum(i - tiles, 0)
    sds = jax.ShapeDtypeStruct
    return pl.pallas_call(
        functools.partial(feed_kernel, tile, chunk, tiles),
        grid=(tiles + chunks,),
        in_specs=[row, row] + [whole(a) for a in (wu, wd, g3, s3, bd, bu, g4, s4)],
        out_specs=[
            row, row,
            pl.BlockSpec((width, chunk), lambda i: (0, late(i))),
            pl.BlockSpec((chunk, width), lambda i: (late(i), 0)),
            pl.BlockSpec((3, width), lambda i: (0, 0)),
            pl.BlockSpec((1, ff), lambda i: (0, 0)),
            pl.BlockSpec((2, ff), lambda i: (0, 0)),
        ],
        out_shape=[
            sds((tokens, width), BF16), sds((tokens, width), F32), sds((width, ff), BF16), sds((ff, width), BF16),
            sds((3, width), F32), sds((1, ff), F32), sds((2, ff), F32),
        ],
        scratch_shapes=[
            pltpu.VMEM((tile, ff), F32), pltpu.VMEM((tile, ff), F32), pltpu.VMEM((tile, ff), F32),
            pltpu.VMEM((ff, tokens), BF16), pltpu.VMEM((tokens, ff), BF16), pltpu.VMEM((width, tokens), BF16),
            pltpu.VMEM((tokens, width), BF16), pltpu.VMEM((tile, width), F32),
            pltpu.VMEM((24, ff), F32), pltpu.VMEM((24, width), F32),
        ],
        compiler_params=pltpu.CompilerParams(vmem_limit_bytes=64000000),
        name="feed_forward",
    )(x1, gd, wu, wd, g3, s3, bd, bu, g4, s4)


MESH = pl.DeviceIdType.MESH
AXES = ("dp", "shard")


class Grid:
    def __init__(self, dp, shard):
        self.ny = dp // 2
        self.nx = self.ny
        self.nz = shard // self.nx

    def here(self):
        dp, shard = lax.axis_index("dp"), lax.axis_index("shard")
        return dp // 2, dp % 2, shard // self.nx, shard % self.nx

    def device(self, y, c, z, x):
        return (y * 2 + c, z * self.nx + x)

    def blocks(self):
        return (self.ny, 2, self.nz, self.nx)


def others(size, mine):
    return [lax.rem(mine + k, size) for k in range(1, size)]


def greet(grid, y, c, z, x):
    barrier = pltpu.get_barrier_semaphore()
    peers = (
        [(y, c, p, x) for p in others(grid.nz, z)]
        + [(y, c, z, p) for p in others(grid.nx, x)]
        + [(p, c, z, x) for p in others(grid.ny, y)]
        + [(y, 1 - c, z, x)]
    )
    for peer in peers:
        pl.semaphore_signal(barrier, inc=1, device_id=grid.device(*peer), device_id_type=MESH)
    pl.semaphore_wait(barrier, len(peers))


class Gather:
    def __init__(self, grid, place, source, target, colour, send, recv, local):
        self.g, self.place = grid, place
        self.source, self.target, self.colour = source, target, colour
        self.send, self.recv, self.local = send, recv, local

    def plan(self, phase):
        g = self.g
        y, c, z, x = self.place
        t = self.target
        if phase == 0:
            return [(self.source, t.at[y, c, z, x], t.at[y, c, p, x], (y, c, p, x), z, p) for p in others(g.nz, z)]
        if phase == 3:
            return [(t.at[:, c], t.at[:, c], t.at[:, 1 - c], (y, 1 - c, z, x), c, 1 - c)]
        along_x = (phase == 1) == (self.colour == 0)
        if along_x:
            cut = (lambda p: t.at[y, c, :, p]) if phase == 1 else (lambda p: t.at[:, c, :, p])
            return [(cut(x), cut(x), cut(p), (y, c, z, p), x, p) for p in others(g.nx, x)]
        cut = (lambda p: t.at[p, c, :, x]) if phase == 1 else (lambda p: t.at[p, c])
        return [(cut(y), cut(y), cut(p), (p, c, z, x), y, p) for p in others(g.ny, y)]

    def go(self, phase, entry):
        src, dst, _, peer, mine, theirs = entry
        return pltpu.make_async_remote_copy(
            src_ref=src, dst_ref=dst, send_sem=self.send.at[phase, theirs], recv_sem=self.recv.at[phase, mine],
            device_id=self.g.device(*peer), device_id_type=MESH)

    def come(self, phase, entry):
        _, _, landed, peer, _, theirs = entry
        return pltpu.make_async_remote_copy(
            src_ref=landed, dst_ref=landed, send_sem=self.send.at[phase, theirs], recv_sem=self.recv.at[phase, theirs],
            device_id=self.g.device(*peer), device_id_type=MESH)

    def own(self):
        y, c, z, x = self.place
        return pltpu.make_async_copy(self.source, self.target.at[y, c, z, x], self.local)

    def start(self, phase):
        if phase == 0:
            self.own().start()
        for entry in self.plan(phase):
            self.go(phase, entry).start()

    def arrive(self, phase):
        if phase == 0:
            self.own().wait()
        for entry in self.plan(phase):
            self.come(phase, entry).wait_recv()

    def drain(self):
        for phase in range(4):
            for entry in self.plan(phase):
                self.go(phase, entry).wait_send()


def in_turn(groups, step, last):
    for tick in range(len(groups) + last - 1):
        for phase in range(1, last + 1):
            i = tick - (phase - 1)
            if 0 <= i < len(groups):
                step(phase, groups[i])


def group_jobs(jobs, plan):
    count = 1 + max(part[3] for part in plan)
    return [[job for job, part in zip(jobs, plan) if part[3] == g] for g in range(count)]


def gather_jobs(grid, place, plan, sources, targets, send, recv, local):
    jobs = []
    for n, (i, cols, colour, _) in enumerate(plan):
        cut = slice(None) if cols is None else pl.ds(*cols)
        jobs.append(
            Gather(grid, place, sources[i].at[:, cut], Cut(targets[i], cut), colour, send.at[n], recv.at[n], local.at[n])
        )
    return jobs


class Cut:
    def __init__(self, ref, cut):
        self.ref, self.cut = ref, cut

    @property
    def at(self):
        return self

    def __getitem__(self, key):
        key = key if isinstance(key, tuple) else (key,)
        key = key + (slice(None),) * (len(self.ref.shape) - 1 - len(key))
        return self.ref.at[key + (self.cut,)]


def gather_kernel(grid, plan, count, *refs):
    sources, targets, (send, recv, local) = refs[:count], refs[count : 2 * count], refs[2 * count :]
    place = grid.here()
    greet(grid, *place)
    jobs = gather_jobs(grid, place, plan, sources, targets, send, recv, local)
    groups = group_jobs(jobs, plan)
    for job in jobs:
        job.start(0)

    def step(phase, group):
        for job in group:
            job.arrive(phase - 1)
        for job in group:
            job.start(phase)

    in_turn(groups, step, 3)
    for job in jobs:
        job.arrive(3)
    for job in jobs:
        job.drain()


def gather_all(grid, pieces, plan, collective_id):
    n = len(pieces)
    wide = max(grid.nx, grid.ny, grid.nz, 2)
    return pl.pallas_call(
        functools.partial(gather_kernel, grid, plan, n),
        out_shape=[jax.ShapeDtypeStruct(grid.blocks() + p.shape, p.dtype) for p in pieces],
        in_specs=[pl.BlockSpec(memory_space=pltpu.VMEM)] * n,
        out_specs=[pl.BlockSpec(memory_space=pl.ANY)] * n,
        scratch_shapes=[
            pltpu.SemaphoreType.DMA((len(plan), 4, wide)),
            pltpu.SemaphoreType.DMA((len(plan), 4, wide)),
            pltpu.SemaphoreType.DMA((len(plan),)),
        ],
        compiler_params=pltpu.CompilerParams(collective_id=collective_id, has_side_effects=True),
        name="gather_parameters",
    )(*pieces)


class Scatter:
    def __init__(self, grid, place, source, target, held, land, colour, send, recv, local):
        self.g, self.place, self.colour = grid, place, colour
        self.source, self.target, self.held, self.land = source, target, held, land
        self.send, self.recv, self.local = send, recv, local

    def along_y(self, phase):
        return (phase == 1) == (self.colour == 0)

    def plan(self, phase):
        g, held, land = self.g, self.held, self.land
        y, c, z, x = self.place
        if phase == 0:
            return [(self.source.at[:, 1 - c], lambda s: land[0], (y, 1 - c, z, x), c, 1 - c)]
        if phase == 3:
            return [(held.at[y, p, x], lambda s: land[3].at[s], (y, c, p, x), z, p) for p in others(g.nz, z)]
        if self.along_y(phase):
            cut = (lambda p: held.at[p]) if phase == 1 else (lambda p: held.at[p, :, x])
            return [(cut(p), lambda s: land[phase].at[s], (p, c, z, x), y, p) for p in others(g.ny, y)]
        cut = (lambda p: held.at[:, :, p]) if phase == 1 else (lambda p: held.at[y, :, p])
        return [(cut(p), lambda s: land[phase].at[s], (y, c, z, p), x, p) for p in others(g.nx, x)]

    def own(self):
        return pltpu.make_async_copy(self.source.at[:, self.place[1]], self.held, self.local)

    def go(self, phase, entry):
        src, spot, peer, mine, theirs = entry
        return pltpu.make_async_remote_copy(
            src_ref=src, dst_ref=spot(mine), send_sem=self.send.at[phase, theirs], recv_sem=self.recv.at[phase, mine],
            device_id=self.g.device(*peer), device_id_type=MESH)

    def come(self, phase, entry):
        src, spot, peer, mine, theirs = entry
        return pltpu.make_async_remote_copy(
            src_ref=spot(theirs), dst_ref=spot(theirs), send_sem=self.send.at[phase, theirs],
            recv_sem=self.recv.at[phase, theirs], device_id=self.g.device(*peer), device_id_type=MESH)

    def start(self, phase):
        if phase == 0:
            self.own().start()
        for entry in self.plan(phase):
            self.go(phase, entry).start()

    def finish(self, phase):
        g, held, land = self.g, self.held, self.land
        y, c, z, x = self.place
        if phase == 0:
            self.own().wait()
        plan = self.plan(phase)
        for entry in plan:
            self.come(phase, entry).wait_recv()
        kind = held.dtype
        f32 = jnp.float32

        def add(at, parts, out=None):
            total = held[at].astype(f32)
            for part in parts:
                total = total + part.astype(f32)
            if out is None:
                held[at] = total.astype(kind)
            else:
                out[...] = total

        slots = [entry[4] for entry in plan]
        if phase == 0:
            def body(i, carry):
                at = (i // (g.nz * g.nx), i // g.nx % g.nz, i % g.nx)
                add(at, [land[0][at]])
                return carry
            lax.fori_loop(0, g.ny * g.nz * g.nx, body, 0)
        elif phase == 3:
            add((y, z, x), [land[3][s] for s in slots], self.target)
        elif phase == 1 and self.along_y(1):
            def body(i, carry):
                add((y, i // g.nx, i % g.nx), [land[1][s, i // g.nx, i % g.nx] for s in slots])
                return carry
            lax.fori_loop(0, g.nz * g.nx, body, 0)
        elif phase == 1:
            def body(i, carry):
                add((i // g.nz, i % g.nz, x), [land[1][s, i // g.nz, i % g.nz] for s in slots])
                return carry
            lax.fori_loop(0, g.ny * g.nz, body, 0)
        else:
            def body(i, carry):
                add((y, i, x), [land[2][s, i] for s in slots])
                return carry
            lax.fori_loop(0, g.nz, body, 0)

    def drain(self):
        for phase in range(4):
            for entry in self.plan(phase):
                self.go(phase, entry).wait_send()


def scatter_scratch(grid, piece, kind, colour):
    ny, nz, nx = grid.ny, grid.nz, grid.nx
    if colour == 0:
        one, two = (ny, nz, nx), (nx, nz)
    else:
        one, two = (nx, ny, nz), (ny, nz)
    return [pltpu.VMEM(s + piece, kind) for s in ((ny, nz, nx), (ny, nz, nx), one, two, (nz,))]


def scatter_jobs(grid, place, plan, sources, targets, bufs, send, recv, local):
    jobs = []
    for n, (i, cols, colour, _) in enumerate(plan):
        cut = slice(None) if cols is None else pl.ds(*cols)
        jobs.append(
            Scatter(grid, place, Cut(sources[i], cut), targets[i].at[:, cut], bufs[5 * n], bufs[5 * n + 1 : 5 * n + 5],
                    colour, send.at[n], recv.at[n], local.at[n])
        )
    return jobs


def scatter_kernel(grid, plan, count, *refs):
    sources, targets = refs[:count], refs[count : 2 * count]
    bufs = refs[2 * count : 2 * count + 5 * len(plan)]
    send, recv, local = refs[2 * count + 5 * len(plan) :]
    place = grid.here()
    greet(grid, *place)
    jobs = scatter_jobs(grid, place, plan, sources, targets, bufs, send, recv, local)
    groups = group_jobs(jobs, plan)
    for job in jobs:
        job.start(0)

    def step(phase, group):
        for job in group:
            job.finish(phase - 1)
            job.start(phase)

    in_turn(groups, step, 3)
    for job in jobs:
        job.finish(3)
    for job in jobs:
        job.drain()


def scatter_buffers(grid, arrays, plan):
    scratch = []
    for i, cols, colour, _ in plan:
        a = arrays[i]
        scratch += scatter_scratch(grid, (a.shape[4], a.shape[5] if cols is None else cols[1]), a.dtype, colour)
    return scratch


def scatter_all(grid, arrays, plan, collective_id):
    n = len(arrays)
    wide = max(grid.nx, grid.ny, grid.nz, 2)
    return pl.pallas_call(
        functools.partial(scatter_kernel, grid, plan, n),
        out_shape=[jax.ShapeDtypeStruct(a.shape[4:], F32) for a in arrays],
        in_specs=[pl.BlockSpec(memory_space=pl.ANY)] * n,
        out_specs=[pl.BlockSpec(memory_space=pltpu.VMEM)] * n,
        scratch_shapes=scatter_buffers(grid, arrays, plan) + [
            pltpu.SemaphoreType.DMA((len(plan), 4, wide)),
            pltpu.SemaphoreType.DMA((len(plan), 4, wide)),
            pltpu.SemaphoreType.DMA((len(plan),)),
        ],
        compiler_params=pltpu.CompilerParams(
            collective_id=collective_id, has_side_effects=True, vmem_limit_bytes=60000000),
        name="scatter_gradients",
    )(*arrays)


PAIR = 128
HALF = 64


def halves():
    lane = lax.broadcasted_iota(jnp.int32, (1, PAIR), 1)
    low = jnp.where(lane < HALF, 1.0, 0.0)
    return low.astype(BF16), (1.0 - low).astype(BF16)


def stack_heads(values):
    low, high = halves()
    return jnp.concatenate([values * low, values * high], axis=0)


def merge_heads(values):
    half = values.shape[0] // 2
    lane = lax.broadcasted_iota(jnp.int32, (half, PAIR), 1)
    return jnp.where(lane < HALF, values[:half], values[half:])


def bias_of(ids):
    length = ids.shape[1]
    across = jnp.broadcast_to(ids.astype(F32), (PAIR, length))
    down = across.T[:, 0:1]
    across = jnp.broadcast_to(across[0:1], (length, length))
    key = lax.broadcasted_iota(jnp.int32, (length, length), 0)
    query = lax.broadcasted_iota(jnp.int32, (length, length), 1)
    met = ((down == across) & (down >= 0.0)) | (key == query)
    return jnp.where(met, 0.0, -1e30)


def mixer_forward_kernel(
    length, x_ref, ids_ref, wq_ref, wk_ref, wv_ref, wo_ref, g1_ref, s1_ref, bq_ref, bv_ref, g2_ref, s2_ref, bo_ref,
    q_ref, k_ref, v_ref, o_ref, total_ref, x1_ref, bias,
):
    step = pl.program_id(0)
    width = x_ref.shape[1]
    pairs = width // PAIR
    part = lax.rem(step, pairs + 2)

    @pl.when(part == 0)
    def _():
        bias[...] = bias_of(ids_ref[0])
        n1, _ = normed_of(x_ref[...].astype(F32))
        a = (n1 * g1_ref[...] + s1_ref[...]).astype(BF16)
        q = ((dot(a, wq_ref[...]) + bq_ref[...]).astype(BF16) * 0.125).astype(BF16)
        k = dot(a, wk_ref[...]).astype(BF16)
        v = (dot(a, wv_ref[...]) + bv_ref[...]).astype(BF16)
        for h in range(pairs):
            cols = slice(h * PAIR, (h + 1) * PAIR)
            q_ref[h], k_ref[h], v_ref[h] = q[:, cols], k[:, cols], v[:, cols]

    @pl.when((part > 0) & (part <= pairs))
    def _():
        h = jnp.clip(part - 1, 0, pairs - 1)
        scores = flipped(stack_heads(k_ref[h]), q_ref[h])
        turned = v_ref[h].T
        mixed = []
        for i in range(2):
            s = scores[i * length : (i + 1) * length] + bias[...]
            peak = jnp.max(s, axis=0, keepdims=True)
            e = jnp.exp(s - peak)
            total = jnp.sum(e, axis=0, keepdims=True)
            total_ref[0, h, i : i + 1, :] = peak + jnp.log(total)
            mixed.append(dot(turned[i * HALF : (i + 1) * HALF], e.astype(BF16)) * (1.0 / total))
        o_ref[h] = jnp.concatenate(mixed, axis=0).T

    @pl.when(part == pairs + 1)
    def _():
        o = jnp.concatenate([o_ref[h] for h in range(pairs)], axis=1)
        n2, _ = normed_of(o)
        b = (n2 * g2_ref[...] + s2_ref[...]).astype(BF16)
        x1_ref[...] = x_ref[...].astype(F32) + dot(b, wo_ref[...]) + bo_ref[...]


def mixer_forward(x, ids, wq, wk, wv, wo, g1, s1, bq, bv, g2, s2, bo):
    rows, _, length = ids.shape
    tokens, width = x.shape
    pairs = width // PAIR
    steps = pairs + 2
    sds = jax.ShapeDtypeStruct
    whole = lambda a: pl.BlockSpec(a.shape, lambda i: (0, 0), pipeline_mode=pl.Buffered(1))
    flat = pl.BlockSpec((length, width), lambda i: (i // steps, 0))
    heads = pl.BlockSpec((pairs, length, PAIR), lambda i: (0, i // steps, 0))
    split = lambda kind: sds((pairs, tokens, PAIR), kind)
    return pl.pallas_call(
        functools.partial(mixer_forward_kernel, length),
        grid=(rows * steps,),
        in_specs=[flat, pl.BlockSpec((1, 1, length), lambda i: (i // steps, 0, 0))]
        + [whole(a) for a in (wq, wk, wv, wo, g1, s1, bq, bv, g2, s2, bo)],
        out_specs=[heads] * 4 + [pl.BlockSpec((1, pairs, 2, length), lambda i: (i // steps, 0, 0, 0)), flat],
        out_shape=[split(BF16)] * 3 + [split(F32), sds((rows, pairs, 2, length), F32), sds((tokens, width), F32)],
        scratch_shapes=[pltpu.VMEM((length, length), F32)],
        compiler_params=pltpu.CompilerParams(vmem_limit_bytes=64000000),
        name="mixer_forward",
    )(x, ids, wq, wk, wv, wo, g1, s1, bq, bv, g2, s2, bo)


def mixer_backward_kernel(
    length, gx1_ref, x_ref, o_ref, q_ref, k_ref, v_ref, total_ref, ids_ref, wq_ref, wk_ref, wv_ref, wo_ref,
    g1_ref, s1_ref, g2_ref, s2_ref,
    gx_ref, dwq_ref, dwk_ref, dwv_ref, dwo_ref, small_ref,
    go, gh, grads, turned_a, turned_b, delta, bias, sums,
):
    step = pl.program_id(0)
    tokens, width = x_ref.shape
    pairs = width // PAIR
    rows = tokens // length
    work = rows * pairs

    @pl.when(step == 0)
    def _():
        sums[...] = jnp.zeros_like(sums)

    @pl.when(step < rows)
    def _():
        at = pl.ds(pl.multiple_of(step * length, length), length)
        gx1 = gx1_ref[at, :]
        low = gx1.astype(BF16)
        gh[at, :] = low
        gb = flipped(low, wo_ref[...])
        o = jnp.concatenate([o_ref[h, at, :] for h in range(pairs)], axis=1)
        n2, r2 = normed_of(o)
        turned_b[:, at] = (n2 * g2_ref[...] + s2_ref[...]).astype(BF16).T
        sums[0:8, :] += eights(gb * n2)
        sums[8:16, :] += eights(gb)
        sums[16:24, :] += eights(low.astype(F32))
        t = gb * g2_ref[...]
        low = (r2 * (t - mean_of(t) - n2 * mean_of(t * n2))).astype(BF16)
        product = low.astype(F32) * o
        for h in range(pairs):
            cols = slice(h * PAIR, (h + 1) * PAIR)
            go[h, at, :] = low[:, cols]
            turned = product[:, cols].T
            delta[h, 0:1, at] = jnp.sum(turned[:HALF], axis=0, keepdims=True)
            delta[h, 1:2, at] = jnp.sum(turned[HALF:], axis=0, keepdims=True)
        n1, _ = normed_of(x_ref[at, :].astype(F32))
        turned_a[:, at] = (n1 * g1_ref[...] + s1_ref[...]).astype(BF16).T

    @pl.when(step == rows)
    def _():
        dwo_ref[...] = dot(turned_b[...], gh[...]).astype(BF16)

    first = rows + 1

    @pl.when((step >= first) & (step < first + work))
    def _():
        i = jnp.clip(step - first, 0, work - 1)
        r, h = i // pairs, lax.rem(i, pairs)
        at = pl.ds(pl.multiple_of(r * length, length), length)

        @pl.when(h == 0)
        def _():
            bias[...] = bias_of(ids_ref[r])

        q, k, v, g = q_ref[h, at, :], k_ref[h, at, :], v_ref[h, at, :], go[h, at, :]
        scores = flipped(stack_heads(k), q)
        back = flipped(stack_heads(v), g)
        turned = k.T
        soft, sharp, found = [], [], []
        for j in range(2):
            cut = slice(j * length, (j + 1) * length)
            p = jnp.exp(scores[cut] + bias[...] - total_ref[r, h, j : j + 1, :])
            ds = (p * (back[cut] - delta[h, j : j + 1, at])).astype(BF16)
            soft.append(p.astype(BF16))
            sharp.append(ds)
            found.append(dot(turned[j * HALF : (j + 1) * HALF], ds))
        grads[2, h, at, :] = merge_heads(dot(jnp.concatenate(soft, axis=0), g)).astype(BF16)
        grads[1, h, at, :] = merge_heads(dot(jnp.concatenate(sharp, axis=0), q)).astype(BF16)
        grads[0, h, at, :] = (jnp.concatenate(found, axis=0).T * 0.125).astype(BF16)

    second = first + work

    def joined(which, at):
        return jnp.concatenate([grads[which, h, at, :] for h in range(pairs)], axis=1)

    @pl.when(step == second)
    def _():
        every = slice(None)
        dwq_ref[...] = dot(turned_a[...], joined(0, every)).astype(BF16)
        dwk_ref[...] = dot(turned_a[...], joined(1, every)).astype(BF16)
        dwv_ref[...] = dot(turned_a[...], joined(2, every)).astype(BF16)

    @pl.when(step > second)
    def _():
        r = jnp.clip(step - second - 1, 0, rows - 1)
        at = pl.ds(pl.multiple_of(r * length, length), length)
        gq, gk, gv = joined(0, at), joined(1, at), joined(2, at)
        ga = flipped(gq, wq_ref[...]) + flipped(gk, wk_ref[...]) + flipped(gv, wv_ref[...])
        n1, r1 = normed_of(x_ref[at, :].astype(F32))
        sums[24:32, :] += eights(ga * n1)
        sums[32:40, :] += eights(ga)
        sums[40:48, :] += eights(gq.astype(F32))
        sums[48:56, :] += eights(gv.astype(F32))
        t = ga * g1_ref[...]
        gx_ref[at, :] = (gx1_ref[at, :] + r1 * (t - mean_of(t) - n1 * mean_of(t * n1))).astype(BF16)
        small_ref[...] = jnp.sum(sums[...].reshape(7, 8, width), axis=1)


def mixer_backward(gx1, x, o, q, k, v, total, ids, wq, wk, wv, wo, g1, s1, g2, s2):
    rows, _, length = ids.shape
    tokens, width = x.shape
    pairs = width // PAIR
    sds = jax.ShapeDtypeStruct
    vmem = pl.BlockSpec(memory_space=pltpu.VMEM)
    return pl.pallas_call(
        functools.partial(mixer_backward_kernel, length),
        grid=(rows + 1 + rows * pairs + 1 + rows,),
        in_specs=[vmem] * 16,
        out_specs=[vmem] * 6,
        out_shape=[sds((tokens, width), BF16)] + [sds((width, width), BF16)] * 4 + [sds((7, width), F32)],
        scratch_shapes=[
            pltpu.VMEM((pairs, tokens, PAIR), BF16), pltpu.VMEM((tokens, width), BF16),
            pltpu.VMEM((3, pairs, tokens, PAIR), BF16), pltpu.VMEM((width, tokens), BF16),
            pltpu.VMEM((width, tokens), BF16), pltpu.VMEM((pairs, 2, tokens), F32),
            pltpu.VMEM((length, length), F32), pltpu.VMEM((56, width), F32),
        ],
        compiler_params=pltpu.CompilerParams(vmem_limit_bytes=64000000),
        name="mixer_backward",
    )(gx1, x, o, q, k, v, total, ids, wq, wk, wv, wo, g1, s1, g2, s2)


MATRICES = ("wq", "wk", "wv", "wo", "wu", "wd")
VECTORS = ("g1", "s1", "bq", "bv", "g2", "s2", "bo", "g3", "s3", "bd", "bu", "g4", "s4")
ORDER = (
    "g1", "s1", "wq", "bq", "wk", "wv", "bv", "g2", "s2", "wo", "bo", "g3", "s3", "wu", "bu", "g4", "s4", "wd", "bd",
)


def pack(vectors):
    size = sum(v.shape[-1] for v in vectors)
    padded = -(-size // 1024) * 1024
    flat, at = 0, 0
    for v in vectors:
        flat = flat + jnp.pad(v, [(0, 0)] * (v.ndim - 1) + [(at, padded - at - v.shape[-1])])
        at += v.shape[-1]
    return flat.reshape(flat.shape[:-1] + (padded // 128, 128))


def halved(i, cols, pieces, colour, group):
    size = cols // pieces
    return [(i, (n * size, size), (colour + n) % 2, group + n) for n in range(pieces)]


def fetch(grid, own):
    pieces = [own[name] for name in MATRICES] + [pack([own[name] for name in VECTORS])]
    plan = [(6, None, 0, 0), (0, None, 0, 0), (1, None, 1, 0), (2, None, 0, 1), (3, None, 1, 1)]
    plan += halved(4, own["wu"].shape[1], 6, 0, 2) + halved(5, own["wd"].shape[1], 6, 1, 2)
    found = gather_all(grid, pieces, plan, 0)
    full = {name: got.reshape(-1, got.shape[-1]) for name, got in zip(MATRICES, found)}
    small = found[-1].reshape(-1, pieces[-1].size)
    at = 0
    for name in VECTORS:
        size = own[name].shape[0]
        full[name] = small[:, at : at + size].reshape(1, -1).astype(F32)
        at += size
    return full


def hand_out(grid, grads, own):
    blocks = grid.blocks()
    count = grid.ny * 2 * grid.nz * grid.nx
    arrays = [grads[name].reshape(blocks + own[name].shape) for name in MATRICES]
    small = pack([grads[name].reshape(count, -1) for name in VECTORS])
    arrays.append(small.reshape(blocks + small.shape[1:]))
    plan = halved(4, own["wu"].shape[1], 6, 0, 0) + halved(5, own["wd"].shape[1], 6, 1, 0)
    plan += [(6, None, 0, 6), (0, None, 0, 6), (1, None, 1, 6), (2, None, 0, 7), (3, None, 1, 7)]
    owned = scatter_all(grid, arrays, plan, 1)
    out = dict(zip(MATRICES, owned))
    small = owned[-1].reshape(-1)
    at = 0
    for name in VECTORS:
        size = own[name].shape[0]
        out[name] = small[at : at + size]
        at += size
    return out


def on_device(grid, inputs, doc_ids, *rest):
    own = dict(zip(ORDER, rest[:-1]))
    width = inputs.shape[-1]
    x = inputs.reshape(-1, width)
    ids = doc_ids.reshape(-1, 1, doc_ids.shape[-1])
    gd = rest[-1].reshape(-1, width)
    p = fetch(grid, own)
    q, k, v, o, total, x1 = mixer_forward(
        x, ids, *(p[n] for n in ("wq", "wk", "wv", "wo", "g1", "s1", "bq", "bv", "g2", "s2", "bo"))
    )
    g = {}
    out, gx1, g["wu"], g["wd"], d3, g["bu"], d4 = feed(
        x1, gd, *(p[n] for n in ("wu", "wd", "g3", "s3", "bd", "bu", "g4", "s4"))
    )
    input_grad, g["wq"], g["wk"], g["wv"], g["wo"], small = mixer_backward(
        gx1, x, o, q, k, v, total, ids, *(p[n] for n in ("wq", "wk", "wv", "wo", "g1", "s1", "g2", "s2"))
    )
    g["g3"], g["s3"], g["bd"] = d3
    g["g4"], g["s4"] = d4
    g["g2"], g["s2"], g["bo"], g["g1"], g["s1"], g["bq"], g["bv"] = small
    got = hand_out(grid, g, own)
    return (out.reshape(inputs.shape), input_grad.reshape(inputs.shape)) + tuple(got[name] for name in ORDER)


def solution(mesh):
    both = ("dp", "shard")
    grid = Grid(mesh.shape["dp"], mesh.shape["shard"])
    rows = P(None, both, None, None)
    params = tuple(P(both, None) if name in MATRICES else P(both) for name in ORDER)
    return jax.shard_map(
        functools.partial(on_device, grid),
        mesh=mesh,
        in_specs=(rows, P(None, both, None)) + params + (rows,),
        out_specs=(rows, rows) + params,
        check_vma=False,
    )
```

time: 546 us -> 330 us (0.60); the launches traced: 537 us -> 330 us
  matrix products: 174 us -> 0 us
  other arithmetic: 64.4 us -> 2.48 us
  Pallas kernels: 254 us -> 301 us
  local copies, waits for them, and re-layouts: 42 us -> 25.5 us
    dot_general x30 -> x0, matrix products: 174 us -> none  [the longest x18 120 us: dot(): lax.dot_general(left, right, (dims, ((), ())), preferred_element_type=F32)]
    pallas_call x2 -> x5, Pallas kernels: 254 us -> 301 us  [the longest x1 92.7 us: gather_all(): pl.pallas_call(functools.partial(gather_kernel, grid, plan, n), out_shape...]
    reduce_sum x14 -> x0, other arithmetic: 38.4 us -> none  [the longest x1 19.1 us: on_device(): g['bu'] = jnp.sum(gu.astype(F32), axis=0)]
    convert_element_type x7 -> x2, other arithmetic: 24.2 us -> 0.17 us  [fetch(): full[name] = small[:, at:at + size].reshape(1, -1).astype(F32)]
    unnamed x193 -> x14, local copies, waits for them, and re-layouts: 21.2 us -> 11 us
    concatenate x2 -> x0, local copies, waits for them, and re-layouts: 9 us -> none  [pack(): flat = jnp.concatenate(vectors, axis=-1)]
    convert_element_type x13, local copies, waits for them, and re-layouts: 2.34 us -> 8.79 us  [fetch(): full[name] = small[:, at:at + size].reshape(1, -1).astype(F32)]
where the time goes in v2:
time: 330 us
  Pallas kernels  301 us (91%)
  local copies, waits for them, and re-layouts  25.5 us (8%)
    pallas_call x1, Pallas kernels, gather_all(): pl.pallas_call(functools.partial(gather_kernel, grid, plan, n), out_shape...  92.7 us
    pallas_call x1, Pallas kernels, scatter_all(): pl.pallas_call(functools.partial(scatter_kernel, grid, plan, n), out_shap...  84.5 us
    pallas_call x1, Pallas kernels, feed(): pl.pallas_call(functools.partial(feed_kernel, tile, chunk, tiles), grid=(...  50.9 us
    pallas_call x1, Pallas kernels, mixer_backward(): pl.pallas_call(functools.partial(mixer_backward_kernel, length), grid=(ro...  45.9 us
    pallas_call x1, Pallas kernels, mixer_forward(): pl.pallas_call(functools.partial(mixer_forward_kernel, length), grid=(row...  26.6 us
    unnamed x14, local copies, waits for them, and re-layouts  11 us
    convert_element_type x13, local copies, waits for them, and re-layouts, fetch(): full[name] = small[:, at:at + size].reshape(1, -1).astype(F32)  8.79 us

profile of v2, /device:TPU:0, one launch (start us, length us, event | category | flops | bytes accessed | tf_op | source)
XLA Modules:
  0.0 329.5 jit_solution(1198346110138162739)
XLA Ops:
  0.7 1.5 add_bitcast_fusion.1.refs_6_
  2.1 92.7 %gather_parameters.1 = (bf16[2,2,4,2,24,768]{5,4,3,2,1,0:T(8,128)(2,1)}, bf16[2,2,4,2,24,768]{5,4,3,2,1,0:T(8,128)(2,1)}, bf16[2,2,4,2,24,768]{5,4,3,2,1,0:T(8,1...) custom-call(bf16[24,768]{1,0:T(8,128)(2,1)} %refs_0_.1, ...), custom_call_target="tpu_custom_call" | custom-call | tf_op jit(solution)/shard_map/gather_parameters/pallas_call | solution.py:317
  94.9 0.9 copy.50
  95.8 0.7 reshape.317.g1_ref
  97.2 0.7 reshape.321.g2_ref
  97.9 0.7 reshape.322.s2_ref
  100.6 26.6 %mixer_forward.1 = (bf16[6,1024,128]{2,1,0:T(8,128)(2,1)}, bf16[6,1024,128]{2,1,0:T(8,128)(2,1)}, bf16[6,1024,128]{2,1,0:T(8,128)(2,1)}, f32[6,1024,128]{2,1,0:T...) custom-call(bf16[1024,768]{1,0:T(8,128)(2,1)} %bitcast.32, s32[2,1,512]{2,1,0:T(1,128)} %ids_ref.3, ...), custom_call_target="tpu_custom_call" | custom-call | tf_op jit(solution)/shard_map/mixer_forward/pallas_call | solution.py:582
  128.5 0.7 reshape.326.bd_ref
  129.2 0.7 reshape.327.bu_ref
  129.9 0.7 reshape.328.g4_ref
  130.6 0.7 reshape.329.s4_ref
  131.3 50.9 %feed_forward.1 = (bf16[1024,768]{1,0:T(8,128)(2,1)}, f32[1024,768]{1,0:T(8,128)}, bf16[768,3072]{1,0:T(8,128)(2,1)}, bf16[3072,768]{1,0:T(8,128)(2,1)}, f32[3,7...) custom-call(f32[1024,768]{1,0:T(8,128)} %get-tuple-element.59.x1_ref, bf16[1024,768]{1,0:T(8,128)(2,1)} %bitcast.46, ...), custom_call_target="tpu_custom_call" | custom-call | tf_op jit(solution)/shard_map/feed_forward/pallas_call | solution.py:135
  182.2 45.9 %mixer_backward.1 = (bf16[1024,768]{1,0:T(8,128)(2,1)}, bf16[768,768]{1,0:T(8,128)(2,1)}, bf16[768,768]{1,0:T(8,128)(2,1)}, bf16[768,768]{1,0:T(8,128)(2,1)}, bf...) custom-call(f32[1024,768]{1,0:T(8,128)} %get-tuple-element.63.gx1_ref, bf16[1024,768]{1,0:T(8,128)(2,1)} %bitcast.33, ...), custom_call_target="tpu_custom_call" | custom-call | tf_op jit(solution)/shard_map/mixer_backward/pallas_call | solution.py:702
  228.2 1.1 slice_reduce_fusion.11
  231.8 0.7 copy.48
  232.5 84.5 %scatter_gradients.1 = (f32[24,768]{1,0:T(8,128)}, f32[24,768]{1,0:T(8,128)}, f32[24,768]{1,0:T(8,128)}, f32[24,768]{1,0:T(8,128)}, f32[24,3072]{1,0:T(8,128)}, /*index=5*/f32[96,768]{1,0:T(8,128)}, f32[8,128]{1,0:T(8,128)}) custom-call(bf16[2,2,4,2,24,768]{5,4,3,2,1,0:T(8,128)(2,1)} %bitcast.47, bf16[2,2,4,2,24,768]{5,4,3,2,1,0:T(8,128)(2,1)} %bitcast.48, ...), custom_call_target="tpu_custom_call" | custom-call | tf_op jit(solution)/shard_map/scatter_gradients/pallas_call | solution.py:480
  317.0 1.7 fusion
  318.7 1.4 fusion.1
  320.1 1.5 copy.57
  321.6 1.5 copy.58
  323.1 1.5 copy.59
  324.6 1.5 copy.60
  326.1 1.7 copy.61
  327.8 1.7 copy.62
  (32 shorter events, 6.7 us)
Async XLA Ops:
  182.2 47.6 %copy-start = (f32[2,3072]{1,0:T(2,128)S(1)}, f32[2,3072]{1,0:T(2,128)}, u32[]{:S(2)}) copy-start(f32[2,3072]{1,0:T(2,128)} %get-tuple-element.79) | copy-start | bytes 73732
  182.2 48.4 %copy-start.1 = (f32[1,3072]{1,0:T(1,128)S(1)}, f32[1,3072]{1,0:T(1,128)}, u32[]{:S(2)}) copy-start(f32[1,3072]{1,0:T(1,128)} %get-tuple-element.78) | copy-start | bytes 36868
  182.2 49.1 %copy-start.2 = (f32[3,768]{1,0:T(4,128)S(1)}, f32[3,768]{1,0:T(4,128)}, u32[]{:S(2)}) copy-start(f32[3,768]{1,0:T(4,128)} %get-tuple-element.77) | copy-start | bytes 27652
